TPU v7x, 32 devices: a whole 2x2x4 slice. The times are simulated.
32 devices in a mesh: dp: 16 (over z, y, core), ctx: 2 (over x).
Axes of the slice: x: 2, y: 2, z: 4, core: 2. Of those that a mesh axis runs over, the one named last changes fastest.
Arguments:
- tokens_in: bfloat16 [32, 512, 768], P('dp', 'ctx'), may hold values from -6 to 6
- live_mask: int32 [32], P('dp'), may hold values from 0 to 1, as said below
- cotangent: bfloat16 [32, 512, 768], P('dp', 'ctx'), may hold values from -6 to 6
- gains: bfloat16 [2, 768], P(None, ('dp', 'ctx')), may hold values from 0.099609375 to 1.8984375
- biases: bfloat16 [6, 768], P(None, ('dp', 'ctx')), may hold values from -3 to 3
- fc_bias: bfloat16 [3072], P(('dp', 'ctx')), may hold values from -3 to 3
- w_qkv: bfloat16 [768, 2304], P(('dp', 'ctx')), may hold values from -0.21875 to 0.21875
- w_out: bfloat16 [768, 768], P(('dp', 'ctx')), may hold values from -0.875 to 0.875
- w_fc: bfloat16 [768, 3072], P(('dp', 'ctx')), may hold values from -0.21875 to 0.21875
- w_proj: bfloat16 [3072, 768], P(('dp', 'ctx')), may hold values from -0.109375 to 0.109375
Outputs:
- block_out: bfloat16 [32, 512, 768], P('dp', 'ctx')
- grad_input: float32 [32, 512, 768], P('dp', 'ctx')
- grad_gains: float32 [2, 768], P(None, ('dp', 'ctx'))
- grad_biases: float32 [6, 768], P(None, ('dp', 'ctx'))
- grad_fc_bias: float32 [3072], P(('dp', 'ctx'))
- grad_w_qkv: float32 [768, 2304], P(('dp', 'ctx'))
- grad_w_out: float32 [768, 768], P(('dp', 'ctx'))
- grad_w_fc: float32 [768, 3072], P(('dp', 'ctx'))
- grad_w_proj: float32 [3072, 768], P(('dp', 'ctx'))
Inputs may be any that keep to these rules, and one draw needn't show every extreme that they name: `live_mask`: the first of each data group's 2 slots always holds a sequence; some groups hold 2 sequences and some fewer in every draw.
All inputs are finite; a program needn't handle non-finite values.
Results may differ from a plain program's by a relative error of at most 0.012.
Values may be sent and summed in bfloat16 or wider, within the bound.
No kernel may reach another device: no remote copies, remote signals or barrier semaphores. Data moves between devices by JAX's collectives and lax.ppermute only.
A program may use at most 192 MiB of HBM per device.

v0:
```python
import jax
import jax.numpy as jnp
from jax import lax
from jax.experimental import pallas as pl
from jax.experimental.pallas import tpu as pltpu
from jax.sharding import PartitionSpec as P


HD = 64
NORM_EPS = 1e-05
SCORE_SCALE = 0.125
MASK_FILL = -1e30
SMALL = 12
PAD = 128
BOTH = ("dp", "ctx")


def layer_norm(values_in, gain, shift):
    center = values_in - jnp.mean(values_in, -1, keepdims=True)
    inv_std = lax.rsqrt(jnp.mean(center * center, -1, keepdims=True) + NORM_EPS)
    normed = center * inv_std
    return (normed * gain + shift, normed, inv_std)


def norm_back(upstream, gain, normed, inv_std):
    scaled = upstream * gain
    return inv_std * (
        scaled
        - jnp.mean(scaled, -1, keepdims=True)
        - normed * jnp.mean(scaled * normed, -1, keepdims=True)
    )


def gelu_back(pre_act, upstream):
    return jax.vjp(lambda values_in: jax.nn.gelu(values_in, approximate=True), pre_act)[1](
        upstream
    )[0]


def rows_product(left, right):
    return lax.dot_general(
        left, right, (((0,), (0,)), ((), ())), preferred_element_type=jnp.float32
    )


def times_transposed(left, right):
    return lax.dot_general(
        left, right, (((1,), (1,)), ((), ())), preferred_element_type=jnp.float32
    )


GRID = (4, 2, 2, 2)


def on_grid():
    return lax.axis_size("dp") == 16 and lax.axis_size("ctx") == 2


def place():
    at = lax.axis_index("dp")
    return at // 4, (at // 2) % 2, at % 2, lax.axis_index("ctx")


def move(block, axis, step):
    pairs = []
    for source in range(32):
        spot = [source // 8, (source // 4) % 2, (source // 2) % 2, source % 2]
        spot[axis] = (spot[axis] + step) % GRID[axis]
        pairs.append((source, ((spot[0] * 2 + spot[1]) * 2 + spot[2]) * 2 + spot[3]))
    return lax.ppermute(block, BOTH, pairs)


def joined(mine, theirs, at, axis):
    first = at == 0
    return jnp.stack([jnp.where(first, mine, theirs), jnp.where(first, theirs, mine)], axis)


def cut_of(columns):
    return columns // 256 * 128


def gather(shard):
    if not on_grid():
        return lax.all_gather(shard, BOTH, axis=0, tiled=False)
    z, y, c, x = place()
    held = [shard] + [move(shard, 0, step) for step in (1, 2, 3)]
    rows = []
    for spot in range(4):
        source = (z - spot) % 4
        row = held[0]
        for step in (1, 2, 3):
            row = jnp.where(source == step, held[step], row)
        rows.append(row)
    ring = jnp.stack(rows, 0)
    cut = cut_of(shard.shape[1])
    left, right = ring[..., :cut], ring[..., cut:]
    left = joined(left, move(left, 1, 1), y, 1)
    right = joined(right, move(right, 3, 1), x, 1)
    left = joined(left, move(left, 3, 1), x, 2)
    right = joined(right, move(right, 1, 1), y, 1)
    half = jnp.concatenate([left, right], -1)
    return joined(half, move(half, 2, 1), c, 2)


def taken(block, at, axis):
    return lax.dynamic_index_in_dim(block, at, axis, keepdims=False)


def added(block, at, axis, arrived):
    total = taken(block, at, axis).astype(jnp.float32) + arrived.astype(jnp.float32)
    return total.astype(jnp.bfloat16)


class Scatter:
    def __init__(self, grads, grid=True):
        devices = lax.axis_size("dp") * lax.axis_size("ctx")
        count, columns = grads.shape[0] // devices, grads.shape[1]
        self.grid = grid and on_grid()
        self.cut = cut_of(columns)
        self.held = grads.reshape((GRID if self.grid else (devices,)) + (count, columns))

    def core(self):
        if self.grid:
            c = place()[2]
            half = added(self.held, c, 2, move(taken(self.held, 1 - c, 2), 2, 1))
            self.held = (half[..., : self.cut], half[..., self.cut :])

    def first(self):
        if self.grid:
            _, y, _, x = place()
            left, right = self.held
            left = added(left, x, 2, move(taken(left, 1 - x, 2), 3, 1))
            right = added(right, y, 1, move(taken(right, 1 - y, 1), 1, 1))
            self.held = (left, right)

    def second(self):
        if self.grid:
            _, y, _, x = place()
            left, right = self.held
            left = added(left, y, 1, move(taken(left, 1 - y, 1), 1, 1))
            right = added(right, x, 1, move(taken(right, 1 - x, 1), 3, 1))
            self.held = jnp.concatenate([left, right], -1)

    def last(self):
        if not self.grid:
            return lax.psum_scatter(self.held, BOTH, scatter_dimension=0, tiled=False).astype(
                jnp.float32
            )
        z = place()[0]
        total = taken(self.held, z, 0).astype(jnp.float32)
        for step in (1, 2, 3):
            sent = taken(self.held, (z + step) % 4, 0)
            total = total + move(sent, 0, step).astype(jnp.float32)
        return total

    def all(self):
        self.core()
        self.first()
        self.second()
        return self.last()


def gate(value, *scatters):
    value, held = lax.optimization_barrier((value, [each.held for each in scatters]))
    for each, now in zip(scatters, held):
        each.held = now
    return value


LANES = 256


def one_head(block, head):
    lane = lax.broadcasted_iota(jnp.int32, block.shape, 1)
    return jnp.where(lane // HD == head, block, jnp.zeros_like(block))


def by_rows(left, right):
    return lax.dot_general(
        left, right, (((1,), (1,)), ((), ())), preferred_element_type=jnp.float32
    )


def own_scores(keys, queries):
    scores = by_rows(keys, queries)
    key_at = lax.broadcasted_iota(jnp.int32, scores.shape, 0)
    query_at = lax.broadcasted_iota(jnp.int32, scores.shape, 1)
    return jnp.where(key_at <= query_at, scores, MASK_FILL)


def far_scores(keys, queries, limit):
    key_at = lax.broadcasted_iota(jnp.int32, (keys.shape[0], 1), 0)
    return by_rows(keys, queries) + jnp.where(key_at < limit, 0.0, MASK_FILL)


def scaled(q):
    return (q.astype(jnp.float32) * SCORE_SCALE).astype(jnp.bfloat16)


def transposed(block):
    return block.astype(jnp.float32).T


def attend_kernel(limit, q_ref, ko_ref, vo_ref, kf_ref, vf_ref, out_ref, log_ref):
    own_values = transposed(vo_ref[0]).astype(jnp.bfloat16)
    far_values = transposed(vf_ref[0]).astype(jnp.bfloat16)
    parts = []
    small = scaled(q_ref[0])
    for head in range(LANES // HD):
        rows = slice(head * HD, (head + 1) * HD)
        queries = one_head(small, head)
        own = own_scores(ko_ref[0], queries)
        far = far_scores(kf_ref[0], queries, limit[0])
        peak = jnp.maximum(jnp.max(own, 0, keepdims=True), jnp.max(far, 0, keepdims=True))
        own = jnp.exp(own - peak)
        far = jnp.exp(far - peak)
        total = jnp.sum(own, 0, keepdims=True) + jnp.sum(far, 0, keepdims=True)
        log_ref[0, 0, head : head + 1, :] = peak + jnp.log(total)
        own = own.astype(jnp.bfloat16)
        far = far.astype(jnp.bfloat16)
        part = jnp.dot(own_values[rows], own, preferred_element_type=jnp.float32) + jnp.dot(
            far_values[rows], far, preferred_element_type=jnp.float32
        )
        parts.append(part * (1.0 / total))
    out_ref[0] = jnp.concatenate(parts, 0).T.astype(jnp.bfloat16)


def block_back(q, keys, values, d_att, attended, logs, scores_of):
    products = (d_att.astype(jnp.float32) * attended.astype(jnp.float32)).T
    keys_across = transposed(keys).astype(jnp.bfloat16)
    d_queries, d_keys, d_values = [], None, None
    small = scaled(q)
    for head in range(LANES // HD):
        rows = slice(head * HD, (head + 1) * HD)
        queries, d_head = one_head(small, head), one_head(d_att, head)
        delta = jnp.sum(products[rows], 0, keepdims=True)
        probs = jnp.exp(scores_of(keys, queries) - logs[head : head + 1])
        d_probs = by_rows(values, d_head)
        d_scores = (probs * (d_probs - delta)).astype(jnp.bfloat16)
        values_term = jnp.dot(
            probs.astype(jnp.bfloat16), d_head, preferred_element_type=jnp.float32
        )
        keys_term = jnp.dot(d_scores, queries, preferred_element_type=jnp.float32)
        d_values = values_term if head == 0 else d_values + values_term
        d_keys = keys_term if head == 0 else d_keys + keys_term
        d_queries.append(jnp.dot(keys_across[rows], d_scores, preferred_element_type=jnp.float32))
    return (jnp.concatenate(d_queries, 0) * SCORE_SCALE).T, d_keys, d_values


def far_kernel(limit, q_ref, k_ref, v_ref, d_ref, o_ref, log_ref, dq_ref, dkv_ref):
    d_queries, d_keys, d_values = block_back(
        q_ref[0], k_ref[0], v_ref[0], d_ref[0], o_ref[0], log_ref[0, 0],
        lambda keys, queries: far_scores(keys, queries, limit[0]),
    )
    dq_ref[0] = d_queries
    dkv_ref[0, 0] = d_keys.astype(jnp.bfloat16)
    dkv_ref[0, 1] = d_values.astype(jnp.bfloat16)


def own_kernel(
    q_ref, k_ref, v_ref, d_ref, o_ref, log_ref, before_ref, dq_ref, sum_ref, dkv_ref
):
    d_queries, d_keys, d_values = block_back(
        q_ref[0], k_ref[0], v_ref[0], d_ref[0], o_ref[0], log_ref[0, 0], own_scores
    )
    d_queries = d_queries + before_ref[0]
    dq_ref[0] = d_queries.astype(jnp.bfloat16)
    sum_ref[0] = jnp.sum(d_queries, 0, keepdims=True)
    dkv_ref[0, 0] = d_keys
    dkv_ref[0, 1] = d_values


def rows_spec(rows, skip=0, slot=0):
    return pl.BlockSpec((1, rows, LANES), lambda p, *_: (slot, 0, p + skip))


def log_spec(span):
    return pl.BlockSpec((1, 1, LANES // HD, span), lambda p, *_: (0, p, 0, 0))


def pair_spec(rows):
    return pl.BlockSpec((1, 2, rows, LANES), lambda p, *_: (0, 0, 0, p))


def attend(limit, queries, near, far, slot):
    _, span, width = queries.shape
    groups, reach = width // LANES, far.shape[1]
    return pl.pallas_call(
        attend_kernel,
        grid_spec=pltpu.PrefetchScalarGridSpec(
            num_scalar_prefetch=1,
            grid=(groups,),
            in_specs=[
                rows_spec(span, 0, slot),
                rows_spec(span, 0, slot),
                rows_spec(span, groups, slot),
                rows_spec(reach),
                rows_spec(reach, groups),
            ],
            out_specs=[rows_spec(span), log_spec(span)],
        ),
        out_shape=[
            jax.ShapeDtypeStruct((1, span, width), jnp.bfloat16),
            jax.ShapeDtypeStruct((1, groups, LANES // HD, span), jnp.float32),
        ],
        name="attend",
    )(limit, queries, near, near, far, far)


def far_back(limit, queries, far, d_att, attended, logs, slot):
    _, span, width = queries.shape
    groups, reach = width // LANES, far.shape[1]
    return pl.pallas_call(
        far_kernel,
        grid_spec=pltpu.PrefetchScalarGridSpec(
            num_scalar_prefetch=1,
            grid=(groups,),
            in_specs=[
                rows_spec(span, 0, slot),
                rows_spec(reach),
                rows_spec(reach, groups),
                rows_spec(span, 0, slot),
                rows_spec(span),
                log_spec(span),
            ],
            out_specs=[rows_spec(span), pair_spec(reach)],
        ),
        out_shape=[
            jax.ShapeDtypeStruct((1, span, width), jnp.float32),
            jax.ShapeDtypeStruct((1, 2, reach, width), jnp.bfloat16),
        ],
        name="far_back",
    )(limit, queries, far, far, d_att, attended, logs)


def own_back(queries, near, d_att, attended, logs, before, slot):
    _, span, width = queries.shape
    groups = width // LANES
    return pl.pallas_call(
        own_kernel,
        grid=(groups,),
        in_specs=[
            rows_spec(span, 0, slot),
            rows_spec(span, 0, slot),
            rows_spec(span, groups, slot),
            rows_spec(span, 0, slot),
            rows_spec(span),
            log_spec(span),
            rows_spec(span),
        ],
        out_specs=[
            rows_spec(span),
            pl.BlockSpec((1, 1, LANES), lambda p: (0, 0, p)),
            pair_spec(span),
        ],
        out_shape=[
            jax.ShapeDtypeStruct((1, span, width), jnp.bfloat16),
            jax.ShapeDtypeStruct((1, 1, width), jnp.float32),
            jax.ShapeDtypeStruct((1, 2, span, width), jnp.float32),
        ],
        name="own_back",
    )(queries, near, near, d_att, attended, logs, before)


def on_device(tokens_in, live_mask, cotangent, gains, biases, fc_bias, w_qkv, w_out, w_fc, w_proj):
    slot_count, span, width = tokens_in.shape
    row_count = slot_count * span
    devices = lax.axis_size("dp") * lax.axis_size("ctx")
    own_cols = width // devices
    units = fc_bias.shape[0] * devices
    per_col = units // width
    paired = lax.axis_size("ctx") == 2

    small = jnp.concatenate([gains.T, biases.T, fc_bias.reshape(own_cols, per_col)], 1)
    small = jnp.pad(small, ((0, 0), (0, PAD - SMALL)))
    first = gather(jnp.concatenate([w_qkv, small], 1)).reshape(width, 3 * width + PAD)
    rest = jnp.concatenate(
        [w_out] + [w_fc[:, i * width : (i + 1) * width] for i in range(per_col)] + [w_proj], 0
    )
    if on_grid():
        other = move(rest, 3, 1)
        rest = joined(rest, other, place()[3], 0)
        rest = lax.all_gather(rest, "dp", axis=0, tiled=True)
    else:
        rest = lax.all_gather(rest, BOTH, axis=0, tiled=False)
    qkv_weight = first[:, : 3 * width]
    small_all = first[:, 3 * width : 3 * width + SMALL].astype(jnp.float32)
    gain_rows = small_all[:, :2].T
    bias_rows = small_all[:, 2:8].T
    fc_shift = small_all[:, 8:].reshape(units)
    out_weight = rest[:, :own_cols].reshape(width, width)
    fc_weight = jnp.concatenate(
        [
            rest[:, (i + 1) * own_cols : (i + 2) * own_cols].reshape(width, width)
            for i in range(per_col)
        ],
        1,
    )
    proj_weight = rest[:, (1 + per_col) * own_cols :].reshape(units, width)

    keep_rows = jnp.repeat(live_mask.astype(jnp.float32), span)[:, None]
    hidden_in = tokens_in.reshape(row_count, width).astype(jnp.float32)
    ln_one, normed_one, inv_one = layer_norm(hidden_in, gain_rows[0], bias_rows[0])
    ln_one_b = ln_one.astype(jnp.bfloat16)
    projected = jnp.dot(ln_one_b, qkv_weight, preferred_element_type=jnp.float32)
    queries = (projected[:, :width] + bias_rows[1]).astype(jnp.bfloat16)
    keys_local = projected[:, width : 2 * width].astype(jnp.bfloat16)
    values_local = (projected[:, 2 * width :] + bias_rows[2]).astype(jnp.bfloat16)
    key_value = jnp.concatenate([keys_local, values_local], 1).reshape(slot_count, span, 2 * width)
    rank = lax.axis_index("ctx")
    limit = (rank * span).reshape(1).astype(jnp.int32)
    queries = queries.reshape(slot_count, span, width)
    before, attended_list, logs = [], [], []
    for slot in range(slot_count):
        block = key_value[slot : slot + 1]
        if paired:
            pairs = [(2 * i, 2 * i + 1) for i in range(devices // 2)]
            before.append(lax.ppermute(block, BOTH, pairs))
        else:
            before.append(lax.all_gather(block, "ctx", axis=1, tiled=True))
    for slot in range(slot_count):
        out, log = attend(limit, queries, key_value, before[slot], slot)
        attended_list.append(out)
        logs.append(log)
    attended = jnp.concatenate(attended_list, 0).reshape(row_count, width)
    after_attn = (
        hidden_in + jnp.dot(attended, out_weight, preferred_element_type=jnp.float32) + bias_rows[3]
    )
    ln_two, normed_two, inv_two = layer_norm(after_attn, gain_rows[1], bias_rows[4])
    ln_two_b = ln_two.astype(jnp.bfloat16)
    pre_act = jnp.dot(ln_two_b, fc_weight, preferred_element_type=jnp.float32) + fc_shift
    activated = jax.nn.gelu(pre_act, approximate=True).astype(jnp.bfloat16)
    final = (
        after_attn
        + jnp.dot(activated, proj_weight, preferred_element_type=jnp.float32)
        + bias_rows[5]
    )
    block_out = (keep_rows * final).astype(jnp.bfloat16).reshape(slot_count, span, width)

    upstream = keep_rows * cotangent.reshape(row_count, width).astype(jnp.float32)
    upstream_b = upstream.astype(jnp.bfloat16)
    sum_proj = Scatter(rows_product(activated, upstream_b).astype(jnp.bfloat16), False)
    out_proj = sum_proj.last()
    d_act = times_transposed(upstream_b, proj_weight)
    d_pre = gelu_back(pre_act, d_act)
    d_pre_b = d_pre.astype(jnp.bfloat16)
    sum_fc = Scatter(rows_product(ln_two_b, d_pre_b).astype(jnp.bfloat16))
    sum_fc.core()
    d_ln_two = times_transposed(d_pre_b, fc_weight)
    d_resid = upstream + norm_back(d_ln_two, gain_rows[1], normed_two, inv_two)
    d_resid_b = d_resid.astype(jnp.bfloat16)
    d_att = times_transposed(d_resid_b, out_weight).astype(jnp.bfloat16)
    d_att = gate(d_att, sum_fc).reshape(slot_count, span, width)
    sum_fc.first()
    d_far, arrived = [], []
    for slot in range(slot_count):
        d_part, terms = far_back(
            limit, queries, before[slot], d_att, attended_list[slot], logs[slot], slot
        )
        d_far.append(d_part)
        if paired:
            back = [(2 * i + 1, 2 * i) for i in range(devices // 2)]
            arrived.append(lax.ppermute(terms, BOTH, back))
        else:
            arrived.append(lax.psum_scatter(terms, "ctx", scatter_dimension=2, tiled=True))
    own_parts = []
    for slot in range(slot_count):
        own_parts.append(
            own_back(queries, key_value, d_att, attended_list[slot], logs[slot], d_far[slot], slot)
        )
    d_queries = jnp.concatenate([part[0] for part in own_parts], 0).reshape(row_count, width)
    query_sums = sum(part[1] for part in own_parts)
    d_queries = gate(d_queries, sum_fc)
    sum_fc.second()
    grad_query = rows_product(ln_one_b, d_queries).astype(jnp.bfloat16)
    grad_out = rows_product(attended, d_resid_b).astype(jnp.bfloat16)
    sum_mid = Scatter(jnp.concatenate([grad_query, grad_out], 1))
    sum_mid.core()
    arrived = gate(arrived, sum_fc, sum_mid)
    sum_mid.first()
    out_fc = sum_fc.last()
    own_terms = jnp.concatenate([part[2] for part in own_parts], 0) + jnp.concatenate(
        arrived, 0
    ).astype(jnp.float32)
    d_keys = own_terms[:, 0].reshape(row_count, width)
    d_values_own = own_terms[:, 1].reshape(row_count, width)
    d_proj_in = jnp.concatenate(
        [d_queries, d_keys.astype(jnp.bfloat16), d_values_own.astype(jnp.bfloat16)], 1
    )
    d_ln_one = times_transposed(d_proj_in, qkv_weight)
    sum_mid.second()
    grad_kv = rows_product(ln_one_b, d_proj_in[:, width:]).astype(jnp.bfloat16)
    d_input = d_resid + norm_back(d_ln_one, gain_rows[0], normed_one, inv_one)
    early = jnp.stack(
        [
            jnp.sum(d_ln_two * normed_two, 0),
            jnp.sum(query_sums, (0, 1)),
            jnp.sum(d_resid, 0),
            jnp.sum(d_ln_two, 0),
            jnp.sum(upstream, 0),
        ],
        0,
    )
    late = jnp.stack(
        [jnp.sum(d_ln_one * normed_one, 0), jnp.sum(d_ln_one, 0), jnp.sum(d_values_own, 0)], 0
    )
    grad_shift = jnp.sum(d_pre, 0).reshape(width, per_col).T
    grad_small = jnp.concatenate([early, grad_shift, late], 0).T.astype(jnp.bfloat16)
    grad_small = jnp.pad(grad_small, ((0, 0), (0, PAD - SMALL)))
    out_mid = sum_mid.last()
    last = Scatter(jnp.concatenate([grad_kv, grad_small], 1)).all()
    out_out = out_mid[:, width:]
    out_qkv = jnp.concatenate([out_mid[:, :width], last[:, : 2 * width]], 1)
    own = last[:, 2 * width : 2 * width + SMALL].T
    order = (10, 1, 11, 2, 3, 4)
    out_gain = jnp.stack([own[9], own[0]], 0)
    out_bias = jnp.stack([own[at] for at in order], 0)
    out_shift = own[5:9].T.reshape(own_cols * per_col)
    return (
        block_out,
        d_input.reshape(slot_count, span, width),
        out_gain,
        out_bias,
        out_shift,
        out_qkv,
        out_out,
        out_fc,
        out_proj,
    )


def solution(mesh):
    in_specs = (
        P("dp", "ctx", None),
        P("dp"),
        P("dp", "ctx", None),
        P(None, ("dp", "ctx")),
        P(None, ("dp", "ctx")),
        P(("dp", "ctx")),
        P(("dp", "ctx"), None),
        P(("dp", "ctx"), None),
        P(("dp", "ctx"), None),
        P(("dp", "ctx"), None),
    )
    out_specs = (
        P("dp", "ctx", None),
        P("dp", "ctx", None),
        P(None, ("dp", "ctx")),
        P(None, ("dp", "ctx")),
        P(("dp", "ctx")),
        P(("dp", "ctx"), None),
        P(("dp", "ctx"), None),
        P(("dp", "ctx"), None),
        P(("dp", "ctx"), None),
    )

    return jax.shard_map(
        on_device, mesh=mesh, in_specs=in_specs, out_specs=out_specs, check_vma=False
    )
```

profile of v0, /device:TPU:0, one launch (start us, length us, event | category | flops | bytes accessed | tf_op | source)
XLA Modules:
  0.0 381.6 jit_solution(17311198618500528901)
XLA Ops:
  15.1 7.8 %collective-permute-done.10 = bf16[216,768]{1,0:T(8,128)(2,1)S(1)} collective-permute-done((bf16[216,768]{1,0:T(8,128)(2,1)S(1)}, bf16[216,768]{1,0:T(8,128)(2,1)S(1)}, u32[]{:S(2)}, u32[]{:S(2)}) %collective-permute-start.10) | collective-permute-done | bytes 331808 | tf_op jit(solution)/shard_map/ppermute | solution.py:70
  31.9 6.4 %collective-permute-done.1 = bf16[24,2432]{1,0:T(8,128)(2,1)S(1)} collective-permute-done((bf16[24,2432]{1,0:T(8,128)(2,1)S(1)}, bf16[24,2432]{1,0:T(8,128)(2,1)S(1)}, u32[]{:S(2)}, u32[]{:S(2)}) %collective-permute-start.1) | collective-permute-done | bytes 116768 | tf_op jit(solution)/shard_map/ppermute | solution.py:70
  41.9 6.3 %collective-permute-done.3 = bf16[4,24,1152]{2,1,0:T(8,128)(2,1)S(1)} collective-permute-done((bf16[4,24,1152]{2,1,0:T(8,128)(2,1)S(1)}, bf16[4,24,1152]{2,1,0:T(8,128)(2,1)S(1)}, u32[]{:S(2)}, u32[]{:S(2)}) %collective-permute-start.3) | collective-permute-done | bytes 221216 | tf_op jit(solution)/shard_map/ppermute | solution.py:70
  50.7 9.4 %collective-permute-done.4 = bf16[4,2,24,1152]{3,2,0,1:T(8,128)(2,1)S(1)} collective-permute-done((bf16[4,2,24,1152]{3,2,0,1:T(8,128)(2,1)S(1)}, bf16[4,2,24,1152]{3,2,0,1:T(8,128)(2,1)S(1)}, u32[]{:S(2)}, u32[]{:S(2)}) %collective-permute-start.4) | collective-permute-done | bytes 442400 | tf_op jit(solution)/shard_map/ppermute | solution.py:70
  64.7 5.9 %collective-permute-done.7 = bf16[4,2,2,24,2432]{4,3,2,1,0:T(8,128)(2,1)} collective-permute-done((bf16[4,2,2,24,2432]{4,3,2,1,0:T(8,128)(2,1)}, bf16[4,2,2,24,2432]{4,3,2,1,0:T(8,128)(2,1)}, u32[]{:S(2)}, u32[]{:S(2)}) %collective-permute-start.7) | collective-permute-done | bytes 1867808 | tf_op jit(solution)/shard_map/ppermute | solution.py:70
  92.8 6.6 %collective-permute-done.9.kf_ref.vf_ref.k_ref.v_ref = bf16[1,256,1536]{2,1,0:T(8,128)(2,1)S(1)} collective-permute-done((bf16[1,256,1536]{2,1,0:T(8,128)(2,1)}, bf16[1,256,1536]{2,1,0:T(8,128)(2,1)S(1)}, u32[]{:S(2)}, u32[]{:S(2)}) %collective-permute-start.9) | collective-permute-done | bytes 786464 | tf_op jit(solution)/shard_map/ppermute | solution.py:418
  100.3 6.0 %attend.3 = (bf16[1,256,768]{2,1,0:T(8,128)(2,1)}, f32[1,3,4,256]{3,2,1,0:T(4,128)}) custom-call(s32[1]{0:T(128)} %bitcast.1.limit, bf16[2,256,768]{2,1,0:T(8,128)(2,1)} %bitcast.259, bf16[2,256,1536]{2,1,0:T(8,128)(2,1)} %bitcast.251, bf16[2,256,1536]{2,1,0:T(8,128)(2,1)} %bitcast.252, bf16[1,256,1536]{2,1,0:T(8,128)(2,1)} %copy-done.2, ...), custom_call_target="tpu_custom_call" | custom-call | tf_op jit(solution)/shard_map/attend/pallas_call | solution.py:288
  106.3 9.4 %collective-permute-done.8.kf_ref.vf_ref.k_ref.v_ref = bf16[1,256,1536]{2,1,0:T(8,128)(2,1)S(1)} collective-permute-done((bf16[1,256,1536]{2,1,0:T(8,128)(2,1)}, bf16[1,256,1536]{2,1,0:T(8,128)(2,1)S(1)}, u32[]{:S(2)}, u32[]{:S(2)}) %collective-permute-start.8) | collective-permute-done | bytes 786464 | tf_op jit(solution)/shard_map/ppermute | solution.py:418
  116.5 5.8 %attend.2 = (bf16[1,256,768]{2,1,0:T(8,128)(2,1)}, f32[1,3,4,256]{3,2,1,0:T(4,128)}) custom-call(s32[1]{0:T(128)} %bitcast.1.limit, bf16[2,256,768]{2,1,0:T(8,128)(2,1)} %bitcast.260, bf16[2,256,1536]{2,1,0:T(8,128)(2,1)} %bitcast.253, bf16[2,256,1536]{2,1,0:T(8,128)(2,1)} %bitcast.254, bf16[1,256,1536]{2,1,0:T(8,128)(2,1)} %copy-done.1, ...), custom_call_target="tpu_custom_call" | custom-call | tf_op jit(solution)/shard_map/attend/pallas_call | solution.py:288
  130.9 4.9 %slice.237 = bf16[32,96,768]{2,1,0:T(8,128)(2,1)S(1)} slice(bf16[32,216,768]{2,1,0:T(8,128)(2,1)} %all-gather.2.cloned.1.call-done), slice={[0:32], [120:216], [0:768]} | slice | bytes 9437184 | tf_op jit(solution)/shard_map/slice | solution.py:399
  135.8 7.2 %fusion.97 = (bf16[3072]{0:T(1024)(128)(2,1)}, bf16[512,3072]{1,0:T(8,128)(2,1)S(1)}) fusion(f32[512,3072]{1,0:T(8,128)S(1)} %fusion.48, f32[3072]{0:T(1024)S(1)} %copy-done.31, bf16[512,768]{1,0:T(8,128)(2,1)S(1)} %bitcast.296, bf16[3072,768]{1,0:T(8,128)(2,1)S(1)} %bitcast.274), kind=kOutput, calls=%fused_computation.255 | convolution fusion | flops 2450519040 | bytes 14960640 | tf_op jit(solution)/shard_map/dot_general | solution.py:47
  159.0 8.9 %convolution_convert_fusion = bf16[3072,768]{1,0:T(8,128)(2,1)} fusion(bf16[512,768]{1,0:T(8,128)(2,1)} %get-tuple-element.129, f32[512,3072]{1,0:T(8,128)} %copy-done.45, f32[3072]{0:T(1024)} %add.358), kind=kOutput, calls=%fused_computation.11 | convolution fusion | flops 2434007040 | bytes 11808768 | tf_op jit(solution)/shard_map/dot_general | solution.py:41
  171.1 9.1 %multiply_convert_fusion.1 = bf16[512,768]{1,0:T(8,128)(2,1)} fusion(f32[512,768]{1,0:T(8,128)S(1)} %copy-done.7, bf16[3072,768]{1,0:T(8,128)(2,1)} %bitcast.275, f32[768]{0:T(1024)S(1)} %copy-done.36, f32[512]{0:T(512)S(1)} %bitcast.311, f32[512,3072]{1,0:T(8,128)} %copy-done.45, f32[3072]{0:T(1024)S(1)} %copy-done.32), kind=kOutput, calls=%fused_computation.79 | convolution fusion | flops 2433220608 | bytes 13386752 | tf_op jit(solution)/shard_map/dot_general | solution.py:435
  184.5 6.4 %far_back.3 = (f32[1,256,768]{2,1,0:T(8,128)}, bf16[1,2,256,768]{3,2,1,0:T(8,128)(2,1)}) custom-call(s32[1]{0:T(128)} %bitcast.1.limit, bf16[2,256,768]{2,1,0:T(8,128)(2,1)} %bitcast.261, bf16[1,256,1536]{2,1,0:T(8,128)(2,1)} %copy-done.2, bf16[1,256,1536]{2,1,0:T(8,128)(2,1)} %copy-done.2, bf16[2,256,768]{2,1,0:T(8,128)(2,1)} %bitcast.265, ...), custom_call_target="tpu_custom_call" | custom-call | tf_op jit(solution)/shard_map/far_back/pallas_call | solution.py:313
  190.9 6.4 %own_back.3 = (bf16[1,256,768]{2,1,0:T(8,128)(2,1)}, f32[1,1,768]{2,1,0:T(1,128)}, f32[1,2,256,768]{3,2,1,0:T(8,128)}) custom-call(bf16[2,256,768]{2,1,0:T(8,128)(2,1)} %bitcast.262, bf16[2,256,1536]{2,1,0:T(8,128)(2,1)} %bitcast.255, bf16[2,256,1536]{2,1,0:T(8,128)(2,1)} %bitcast.256, bf16[2,256,768]{2,1,0:T(8,128)(2,1)} %bitcast.266, ...), custom_call_target="tpu_custom_call" | custom-call | tf_op jit(solution)/shard_map/own_back/pallas_call | solution.py:339
  197.3 6.0 %far_back.2 = (f32[1,256,768]{2,1,0:T(8,128)}, bf16[1,2,256,768]{3,2,1,0:T(8,128)(2,1)}) custom-call(s32[1]{0:T(128)} %bitcast.1.limit, bf16[2,256,768]{2,1,0:T(8,128)(2,1)} %bitcast.263, bf16[1,256,1536]{2,1,0:T(8,128)(2,1)} %copy-done.1, bf16[1,256,1536]{2,1,0:T(8,128)(2,1)} %copy-done.1, bf16[2,256,768]{2,1,0:T(8,128)(2,1)} %bitcast.267, ...), custom_call_target="tpu_custom_call" | custom-call | tf_op jit(solution)/shard_map/far_back/pallas_call | solution.py:313
  203.3 6.5 %own_back.2 = (bf16[1,256,768]{2,1,0:T(8,128)(2,1)}, f32[1,1,768]{2,1,0:T(1,128)}, f32[1,2,256,768]{3,2,1,0:T(8,128)}) custom-call(bf16[2,256,768]{2,1,0:T(8,128)(2,1)} %bitcast.264, bf16[2,256,1536]{2,1,0:T(8,128)(2,1)} %bitcast.257, bf16[2,256,1536]{2,1,0:T(8,128)(2,1)} %bitcast.258, bf16[2,256,768]{2,1,0:T(8,128)(2,1)} %bitcast.268, ...), custom_call_target="tpu_custom_call" | custom-call | tf_op jit(solution)/shard_map/own_back/pallas_call | solution.py:339
  214.5 4.4 %collective-permute-start.12 = (bf16[4,2,24,1536]{3,2,0,1:T(8,128)(2,1)}, bf16[4,2,24,1536]{3,2,0,1:T(8,128)(2,1)}, u32[]{:S(2)}, u32[]{:S(2)}) collective-permute-start(bf16[4,2,24,1536]{3,2,0,1:T(8,128)(2,1)} %dynamic-slice_bitcast_fusion.3), channel_id=1, source_target_pairs={{0,1},{1,0},{2,3},{3,2},{4,5},{5,4},{6,7},{7,6},{8,9},{9,8},{10,11... | collective-permute-start | bytes 1769480 | tf_op jit(solution)/shard_map/ppermute | solution.py:70
  223.0 49.1 %collective-permute-done.12 = bf16[4,2,24,1536]{3,2,0,1:T(8,128)(2,1)} collective-permute-done((bf16[4,2,24,1536]{3,2,0,1:T(8,128)(2,1)}, bf16[4,2,24,1536]{3,2,0,1:T(8,128)(2,1)}, u32[]{:S(2)}, u32[]{:S(2)}) %collective-permute-start.12) | collective-permute-done | bytes 589856 | tf_op jit(solution)/shard_map/ppermute | solution.py:70
  279.0 4.4 %copy.96 = bf16[768,1536]{1,0:T(8,128)(2,1)} copy(bf16[768,1536]{0,1:T(8,128)(2,1)} %pad_maximum_fusion.2) | data formatting | bytes 4718592 | tf_op jit(solution)/shard_map/concatenate | solution.py:477
  310.7 7.3 %collective-permute-start.35 = (bf16[24,3072]{1,0:T(8,128)(2,1)S(1)}, bf16[24,3072]{1,0:T(8,128)(2,1)S(1)}, u32[]{:S(2)}, u32[]{:S(2)}) collective-permute-start(bf16[24,3072]{1,0:T(8,128)(2,1)S(1)} %get-tuple-element.136), channel_id=1, source_target_pairs={{0,16},{1,17},{2,18},{3,19},{4,20},{5,21},{6,22},{7,23},{8,24},{9,... | collective-permute-start | bytes 442376 | tf_op jit(solution)/shard_map/ppermute | solution.py:70
  322.3 9.2 %collective-permute-done.35 = bf16[24,3072]{1,0:T(8,128)(2,1)S(1)} collective-permute-done((bf16[24,3072]{1,0:T(8,128)(2,1)S(1)}, bf16[24,3072]{1,0:T(8,128)(2,1)S(1)}, u32[]{:S(2)}, u32[]{:S(2)}) %collective-permute-start.35) | collective-permute-done | bytes 147488 | tf_op jit(solution)/shard_map/ppermute | solution.py:70
  333.5 4.2 %collective-permute-done.28 = bf16[4,24,768]{2,1,0:T(8,128)(2,1)S(1)} collective-permute-done((bf16[4,24,768]{2,1,0:T(8,128)(2,1)S(1)}, bf16[4,24,768]{2,1,0:T(8,128)(2,1)S(1)}, u32[]{:S(2)}, u32[]{:S(2)}) %collective-permute-start.28) | collective-permute-done | bytes 147488 | tf_op jit(solution)/shard_map/ppermute | solution.py:70
  349.6 5.9 %collective-permute-done.22 = bf16[4,2,24,896]{3,2,1,0:T(8,128)(2,1)S(1)} collective-permute-done((bf16[4,2,24,896]{3,2,1,0:T(8,128)(2,1)S(1)}, bf16[4,2,24,896]{3,2,1,0:T(8,128)(2,1)S(1)}, u32[]{:S(2)}, u32[]{:S(2)}) %collective-permute-start.22) | collective-permute-done | bytes 344096 | tf_op jit(solution)/shard_map/ppermute | solution.py:70
  (304 shorter events, 162.7 us)
Async XLA Ops:
  7.2 116.3 %all-gather.2.cloned.1.call-start = ((), (), s32[]{:S(2)}) async-start(), calls=%async_computation.1 | async-start | bytes 11280384 | tf_op jit(solution)/shard_map/all_gather | solution.py:383
  12.1 10.8 %collective-permute-start.10 = (bf16[216,768]{1,0:T(8,128)(2,1)S(1)}, bf16[216,768]{1,0:T(8,128)(2,1)S(1)}, u32[]{:S(2)}, u32[]{:S(2)}) collective-permute-start(bf16[216,768]{1,0:T(8,128)(2,1)S(1)} %constant_dynamic-update-slice_fusion), channel_id=1, source_target_pairs={{0,1},{1,0},{2,3},{3,2},{4,5},{5,4},{6,7},{7,6},{8,9},{9,8},{10,11... | collective-permute-start | bytes 995336 | tf_op jit(solution)/shard_map/ppermute | solution.py:70
  23.9 349.0 %reduce-scatter.2.cloned.1.call-start = ((), (), s32[]{:S(2)}) async-start(), calls=%async_computation.2 | async-start | bytes 4866048 | tf_op jit(solution)/shard_map/reduce_scatter | solution.py:146
  28.3 10.0 %collective-permute-start.1 = (bf16[24,2432]{1,0:T(8,128)(2,1)S(1)}, bf16[24,2432]{1,0:T(8,128)(2,1)S(1)}, u32[]{:S(2)}, u32[]{:S(2)}) collective-permute-start(bf16[24,2432]{1,0:T(8,128)(2,1)S(1)} %pad_maximum_fusion.18), channel_id=1, source_target_pairs={{0,16},{1,17},{2,18},{3,19},{4,20},{5,21},{6,22},{7,23},{8,24},{9,... | collective-permute-start | bytes 350216 | tf_op jit(solution)/shard_map/ppermute | solution.py:70
  28.3 10.0 %collective-permute-start.2 = (bf16[24,2432]{1,0:T(8,128)(2,1)S(1)}, bf16[24,2432]{1,0:T(8,128)(2,1)S(1)}, u32[]{:S(2)}, u32[]{:S(2)}) collective-permute-start(bf16[24,2432]{1,0:T(8,128)(2,1)S(1)} %pad_maximum_fusion.18), channel_id=1, source_target_pairs={{0,8},{1,9},{2,10},{3,11},{4,12},{5,13},{6,14},{7,15},{8,16},{9,17... | collective-permute-start | bytes 350216 | tf_op jit(solution)/shard_map/ppermute | solution.py:70
  38.6 9.7 %collective-permute-start.3 = (bf16[4,24,1152]{2,1,0:T(8,128)(2,1)S(1)}, bf16[4,24,1152]{2,1,0:T(8,128)(2,1)S(1)}, u32[]{:S(2)}, u32[]{:S(2)}) collective-permute-start(bf16[4,24,1152]{2,1,0:T(8,128)(2,1)S(1)} %pad_maximum_fusion.16), channel_id=1, source_target_pairs={{0,4},{1,5},{2,6},{3,7},{4,0},{5,1},{6,2},{7,3},{8,12},{9,13},{10,... | collective-permute-start | bytes 663560 | tf_op jit(solution)/shard_map/ppermute | solution.py:70
  40.3 9.6 %collective-permute-start.5 = (bf16[4,24,1280]{2,1,0:T(8,128)(2,1)S(1)}, bf16[4,24,1280]{2,1,0:T(8,128)(2,1)S(1)}, u32[]{:S(2)}, u32[]{:S(2)}) collective-permute-start(bf16[4,24,1280]{2,1,0:T(8,128)(2,1)S(1)} %pad_maximum_fusion.13), channel_id=1, source_target_pairs={{0,1},{1,0},{2,3},{3,2},{4,5},{5,4},{6,7},{7,6},{8,9},{9,8},{10,11... | collective-permute-start | bytes 737288 | tf_op jit(solution)/shard_map/ppermute | solution.py:70
  48.4 11.7 %collective-permute-start.4 = (bf16[4,2,24,1152]{3,2,0,1:T(8,128)(2,1)S(1)}, bf16[4,2,24,1152]{3,2,0,1:T(8,128)(2,1)S(1)}, u32[]{:S(2)}, u32[]{:S(2)}) collective-permute-start(bf16[4,2,24,1152]{3,2,0,1:T(8,128)(2,1)S(1)} %pad_maximum_fusion.12), channel_id=1, source_target_pairs={{0,1},{1,0},{2,3},{3,2},{4,5},{5,4},{6,7},{7,6},{8,9},{9,8},{10,11... | collective-permute-start | bytes 1327112 | tf_op jit(solution)/shard_map/ppermute | solution.py:70
  50.1 12.5 %collective-permute-start.6 = (bf16[4,2,24,1280]{3,2,1,0:T(8,128)(2,1)S(1)}, bf16[4,2,24,1280]{3,2,1,0:T(8,128)(2,1)S(1)}, u32[]{:S(2)}, u32[]{:S(2)}) collective-permute-start(bf16[4,2,24,1280]{3,2,1,0:T(8,128)(2,1)S(1)} %pad_maximum_fusion.11), channel_id=1, source_target_pairs={{0,4},{1,5},{2,6},{3,7},{4,0},{5,1},{6,2},{7,3},{8,12},{9,13},{10,... | collective-permute-start | bytes 1474568 | tf_op jit(solution)/shard_map/ppermute | solution.py:70
  79.8 19.6 %collective-permute-start.9 = (bf16[1,256,1536]{2,1,0:T(8,128)(2,1)}, bf16[1,256,1536]{2,1,0:T(8,128)(2,1)S(1)}, u32[]{:S(2)}, u32[]{:S(2)}) collective-permute-start(bf16[1,256,1536]{2,1,0:T(8,128)(2,1)} %get-tuple-element.122), channel_id=1, source_target_pairs={{0,1},{2,3},{4,5},{6,7},{8,9},{10,11},{12,13},{14,15},{16,17},{18,... | collective-permute-start | bytes 2359304 | tf_op jit(solution)/shard_map/ppermute | solution.py:418
  81.2 34.4 %collective-permute-start.8 = (bf16[1,256,1536]{2,1,0:T(8,128)(2,1)}, bf16[1,256,1536]{2,1,0:T(8,128)(2,1)S(1)}, u32[]{:S(2)}, u32[]{:S(2)}) collective-permute-start(bf16[1,256,1536]{2,1,0:T(8,128)(2,1)} %get-tuple-element.121), channel_id=1, source_target_pairs={{0,1},{2,3},{4,5},{6,7},{8,9},{10,11},{12,13},{14,15},{16,17},{18,... | collective-permute-start | bytes 2359304 | tf_op jit(solution)/shard_map/ppermute | solution.py:418
  153.1 27.2 %collective-permute-start.11 = (bf16[4,2,2,24,3072]{4,3,0,2,1:T(8,128)(2,1)}, bf16[4,2,2,24,3072]{4,3,0,2,1:T(8,128)(2,1)}, u32[]{:S(2)}, u32[]{:S(2)}) collective-permute-start(bf16[4,2,2,24,3072]{4,3,0,2,1:T(8,128)(2,1)} %bitcast.250), channel_id=1, source_target_pairs={{0,2},{1,3},{2,0},{3,1},{4,6},{5,7},{6,4},{7,5},{8,10},{9,11},{10,... | collective-permute-start | bytes 7077896 | tf_op jit(solution)/shard_map/ppermute | solution.py:70
  209.8 79.4 %collective-permute-start.14 = (bf16[1,2,256,768]{3,2,1,0:T(8,128)(2,1)}, bf16[1,2,256,768]{3,2,1,0:T(8,128)(2,1)}, u32[]{:S(2)}, u32[]{:S(2)}) collective-permute-start(bf16[1,2,256,768]{3,2,1,0:T(8,128)(2,1)} %get-tuple-element.48), channel_id=1, source_target_pairs={{1,0},{3,2},{5,4},{7,6},{9,8},{11,10},{13,12},{15,14},{17,16},{19,... | collective-permute-start | bytes 2359304 | tf_op jit(solution)/shard_map/ppermute | solution.py:463
  211.2 78.0 %collective-permute-start.15 = (bf16[1,2,256,768]{3,2,1,0:T(8,128)(2,1)}, bf16[1,2,256,768]{3,2,1,0:T(8,128)(2,1)}, u32[]{:S(2)}, u32[]{:S(2)}) collective-permute-start(bf16[1,2,256,768]{3,2,1,0:T(8,128)(2,1)} %get-tuple-element.49), channel_id=1, source_target_pairs={{1,0},{3,2},{5,4},{7,6},{9,8},{11,10},{13,12},{15,14},{17,16},{19,... | collective-permute-start | bytes 2359304 | tf_op jit(solution)/shard_map/ppermute | solution.py:463
  214.5 57.6 %collective-permute-start.12 = (bf16[4,2,24,1536]{3,2,0,1:T(8,128)(2,1)}, bf16[4,2,24,1536]{3,2,0,1:T(8,128)(2,1)}, u32[]{:S(2)}, u32[]{:S(2)}) collective-permute-start(bf16[4,2,24,1536]{3,2,0,1:T(8,128)(2,1)} %dynamic-slice_bitcast_fusion.3), channel_id=1, source_target_pairs={{0,1},{1,0},{2,3},{3,2},{4,5},{5,4},{6,7},{7,6},{8,9},{9,8},{10,11... | collective-permute-start | bytes 1769480 | tf_op jit(solution)/shard_map/ppermute | solution.py:70
  220.8 52.7 %collective-permute-start.13 = (bf16[4,2,24,1536]{3,2,0,1:T(8,128)(2,1)}, bf16[4,2,24,1536]{3,2,0,1:T(8,128)(2,1)}, u32[]{:S(2)}, u32[]{:S(2)}) collective-permute-start(bf16[4,2,24,1536]{3,2,0,1:T(8,128)(2,1)} %dynamic-slice_bitcast_fusion.2), channel_id=1, source_target_pairs={{0,4},{1,5},{2,6},{3,7},{4,0},{5,1},{6,2},{7,3},{8,12},{9,13},{10,... | collective-permute-start | bytes 1769480 | tf_op jit(solution)/shard_map/ppermute | solution.py:70
  275.8 9.2 %collective-permute-start.17 = (bf16[4,24,1536]{2,1,0:T(8,128)(2,1)}, bf16[4,24,1536]{2,1,0:T(8,128)(2,1)}, u32[]{:S(2)}, u32[]{:S(2)}) collective-permute-start(bf16[4,24,1536]{2,1,0:T(8,128)(2,1)} %dynamic-slice_bitcast_fusion.8), channel_id=1, source_target_pairs={{0,1},{1,0},{2,3},{3,2},{4,5},{5,4},{6,7},{7,6},{8,9},{9,8},{10,11... | collective-permute-start | bytes 884744 | tf_op jit(solution)/shard_map/ppermute | solution.py:70
  276.5 9.7 %collective-permute-start.16 = (bf16[4,24,1536]{2,1,0:T(8,128)(2,1)}, bf16[4,24,1536]{2,1,0:T(8,128)(2,1)}, u32[]{:S(2)}, u32[]{:S(2)}) collective-permute-start(bf16[4,24,1536]{2,1,0:T(8,128)(2,1)} %dynamic-slice_bitcast_fusion.9), channel_id=1, source_target_pairs={{0,4},{1,5},{2,6},{3,7},{4,0},{5,1},{6,2},{7,3},{8,12},{9,13},{10,... | collective-permute-start | bytes 884744 | tf_op jit(solution)/shard_map/ppermute | solution.py:70
  308.3 32.2 %collective-permute-start.19 = (bf16[4,2,2,24,1664]{4,3,2,1,0:T(8,128)(2,1)S(1)}, bf16[4,2,2,24,1664]{4,3,2,1,0:T(8,128)(2,1)S(1)}, u32[]{:S(2)}, u32[]{:S(2)}) collective-permute-start(bf16[4,2,2,24,1664]{4,3,2,1,0:T(8,128)(2,1)S(1)} %dynamic-slice_bitcast_fusion), channel_id=1, source_target_pairs={{0,2},{1,3},{2,0},{3,1},{4,6},{5,7},{6,4},{7,5},{8,10},{9,11},{10,... | collective-permute-start | bytes 3833864 | tf_op jit(solution)/shard_map/ppermute | solution.py:70
  308.5 23.8 %collective-permute-start.27 = (bf16[4,2,24,768]{3,2,0,1:T(8,128)(2,1)S(1)}, bf16[4,2,24,768]{3,2,0,1:T(8,128)(2,1)S(1)}, u32[]{:S(2)}, u32[]{:S(2)}) collective-permute-start(bf16[4,2,24,768]{3,2,0,1:T(8,128)(2,1)S(1)} %dynamic-slice_bitcast_fusion.6), channel_id=1, source_target_pairs={{0,1},{1,0},{2,3},{3,2},{4,5},{5,4},{6,7},{7,6},{8,9},{9,8},{10,11... | collective-permute-start | bytes 884744 | tf_op jit(solution)/shard_map/ppermute | solution.py:70
  310.7 11.1 %collective-permute-start.36 = (bf16[24,3072]{1,0:T(8,128)(2,1)S(1)}, bf16[24,3072]{1,0:T(8,128)(2,1)S(1)}, u32[]{:S(2)}, u32[]{:S(2)}) collective-permute-start(bf16[24,3072]{1,0:T(8,128)(2,1)S(1)} %get-tuple-element.135), channel_id=1, source_target_pairs={{0,24},{1,25},{2,26},{3,27},{4,28},{5,29},{6,30},{7,31},{8,0},{9,1... | collective-permute-start | bytes 442376 | tf_op jit(solution)/shard_map/ppermute | solution.py:70
  310.7 20.8 %collective-permute-start.35 = (bf16[24,3072]{1,0:T(8,128)(2,1)S(1)}, bf16[24,3072]{1,0:T(8,128)(2,1)S(1)}, u32[]{:S(2)}, u32[]{:S(2)}) collective-permute-start(bf16[24,3072]{1,0:T(8,128)(2,1)S(1)} %get-tuple-element.136), channel_id=1, source_target_pairs={{0,16},{1,17},{2,18},{3,19},{4,20},{5,21},{6,22},{7,23},{8,24},{9,... | collective-permute-start | bytes 442376 | tf_op jit(solution)/shard_map/ppermute | solution.py:70
  318.0 13.5 %collective-permute-start.34 = (bf16[24,3072]{1,0:T(8,128)(2,1)S(1)}, bf16[24,3072]{1,0:T(8,128)(2,1)S(1)}, u32[]{:S(2)}, u32[]{:S(2)}) collective-permute-start(bf16[24,3072]{1,0:T(8,128)(2,1)S(1)} %get-tuple-element.134), channel_id=1, source_target_pairs={{0,8},{1,9},{2,10},{3,11},{4,12},{5,13},{6,14},{7,15},{8,16},{9,17... | collective-permute-start | bytes 442376 | tf_op jit(solution)/shard_map/ppermute | solution.py:70
  321.7 11.3 %collective-permute-start.29 = (bf16[4,2,24,768]{3,2,1,0:T(8,128)(2,1)S(1)}, bf16[4,2,24,768]{3,2,1,0:T(8,128)(2,1)S(1)}, u32[]{:S(2)}, u32[]{:S(2)}) collective-permute-start(bf16[4,2,24,768]{3,2,1,0:T(8,128)(2,1)S(1)} %dynamic-slice_bitcast_fusion.5), channel_id=1, source_target_pairs={{0,4},{1,5},{2,6},{3,7},{4,0},{5,1},{6,2},{7,3},{8,12},{9,13},{10,... | collective-permute-start | bytes 884744 | tf_op jit(solution)/shard_map/ppermute | solution.py:70
  (61 other events, 432.6 us)
Sparse Core Ops, SparseCore 0:
  24.1 91.7 all-gather.1
  168.0 120.1 reduce-scatter.1
where the time goes:
time: 389 us; the launch traced here: 382 us
  waiting for transfers between devices  140 us (36%)
  local copies, waits for them, and re-layouts  55.8 us (14%)
  matrix products  47.1 us (12%)
  starting transfers between devices  46.7 us (12%)
  other arithmetic  39.6 us (10%)
  Pallas kernels  37.1 us (10%)
  between operations  15.3 us (4%)
    ppermute x33, waiting for transfers between devices, move(): return lax.ppermute(block, BOTH, pairs)  124 us
    ppermute x33, starting transfers between devices, move(): return lax.ppermute(block, BOTH, pairs)  41.1 us
    dot_general x5, matrix products, rows_product(): lax.dot_general(left, right, (((0,), (0,)), ((), ())), preferred_element_...  17 us
    ppermute x2, waiting for transfers between devices, on_device(): before.append(lax.ppermute(block, BOTH, pairs))  16 us
    dot_general x4, matrix products, times_transposed(): lax.dot_general(left, right, (((1,), (1,)), ((), ())), preferred_element_...  15.3 us
    pallas_call x2, Pallas kernels, own_back(): pl.pallas_call(own_kernel, grid=(groups,), in_specs=[rows_spec(span, 0, s...  12.9 us
    pallas_call x2, Pallas kernels, far_back(): pl.pallas_call(far_kernel, grid_spec=pltpu.PrefetchScalarGridSpec(num_sca...  12.4 us
    pallas_call x2, Pallas kernels, attend(): pl.pallas_call(attend_kernel, grid_spec=pltpu.PrefetchScalarGridSpec(num_...  11.8 us
  transfers between devices with their start and end apart: 39, of which 20 were waited for; matrix products, arithmetic and copies ran while one was open for 26% of the time, Pallas kernels for 10%

commit v1 on v0

--- a/solution.py
+++ b/solution.py
@@ -106,44 +106,48 @@
     return lax.dynamic_index_in_dim(block, at, axis, keepdims=False)
 
 
+def summed(mine, arrived):
+    return (mine.astype(jnp.float32) + arrived.astype(jnp.float32)).astype(jnp.bfloat16)
+
+
 def added(block, at, axis, arrived):
-    total = taken(block, at, axis).astype(jnp.float32) + arrived.astype(jnp.float32)
-    return total.astype(jnp.bfloat16)
+    return summed(taken(block, at, axis), arrived)
 
 
 class Scatter:
-    def __init__(self, grads, grid=True):
+    def __init__(self, pieces, flat=False, y_first=True):
         devices = lax.axis_size("dp") * lax.axis_size("ctx")
-        count, columns = grads.shape[0] // devices, grads.shape[1]
-        self.grid = grid and on_grid()
-        self.cut = cut_of(columns)
-        self.held = grads.reshape((GRID if self.grid else (devices,)) + (count, columns))
+        self.grid = on_grid() and not flat
+        self.y_first = y_first
+        lead = GRID if self.grid else (devices,)
+        self.held = [
+            piece.reshape(lead + (piece.shape[0] // devices, piece.shape[1])) for piece in pieces
+        ]
 
     def core(self):
         if self.grid:
             c = place()[2]
-            half = added(self.held, c, 2, move(taken(self.held, 1 - c, 2), 2, 1))
-            self.held = (half[..., : self.cut], half[..., self.cut :])
+            sent = jnp.concatenate([taken(piece, 1 - c, 2) for piece in self.held], -1)
+            mine = jnp.concatenate([taken(piece, c, 2) for piece in self.held], -1)
+            self.held = summed(mine, move(sent, 2, 1))
+
+    def pair(self, axis, at, dim):
+        self.held = added(self.held, at, dim, move(taken(self.held, 1 - at, dim), axis, 1))
 
     def first(self):
         if self.grid:
             _, y, _, x = place()
-            left, right = self.held
-            left = added(left, x, 2, move(taken(left, 1 - x, 2), 3, 1))
-            right = added(right, y, 1, move(taken(right, 1 - y, 1), 1, 1))
-            self.held = (left, right)
+            self.pair(*((1, y, 1) if self.y_first else (3, x, 2)))
 
     def second(self):
         if self.grid:
             _, y, _, x = place()
-            left, right = self.held
-            left = added(left, y, 1, move(taken(left, 1 - y, 1), 1, 1))
-            right = added(right, x, 1, move(taken(right, 1 - x, 1), 3, 1))
-            self.held = jnp.concatenate([left, right], -1)
+            self.pair(*((3, x, 1) if self.y_first else (1, y, 1)))
 
     def last(self):
         if not self.grid:
-            return lax.psum_scatter(self.held, BOTH, scatter_dimension=0, tiled=False).astype(
+            whole = jnp.concatenate(self.held, -1)
+            return lax.psum_scatter(whole, BOTH, scatter_dimension=0, tiled=False).astype(
                 jnp.float32
             )
         z = place()[0]
@@ -152,12 +156,6 @@
             sent = taken(self.held, (z + step) % 4, 0)
             total = total + move(sent, 0, step).astype(jnp.float32)
         return total
-
-    def all(self):
-        self.core()
-        self.first()
-        self.second()
-        return self.last()
 
 
 def gate(value, *scatters):
@@ -418,6 +416,11 @@
             before.append(lax.ppermute(block, BOTH, pairs))
         else:
             before.append(lax.all_gather(block, "ctx", axis=1, tiled=True))
+    upstream = keep_rows * cotangent.reshape(row_count, width).astype(jnp.float32)
+    upstream_b = upstream.astype(jnp.bfloat16)
+    waited = (before[0], key_value, queries, fc_shift, upstream_b, bias_rows, jnp.sum(upstream, 0))
+    waited = lax.optimization_barrier(waited)
+    before[0], key_value, queries, fc_shift, upstream_b, bias_rows, upstream_sum = waited
     for slot in range(slot_count):
         out, log = attend(limit, queries, key_value, before[slot], slot)
         attended_list.append(out)
@@ -435,16 +438,13 @@
         + jnp.dot(activated, proj_weight, preferred_element_type=jnp.float32)
         + bias_rows[5]
     )
-    block_out = (keep_rows * final).astype(jnp.bfloat16).reshape(slot_count, span, width)
-
-    upstream = keep_rows * cotangent.reshape(row_count, width).astype(jnp.float32)
-    upstream_b = upstream.astype(jnp.bfloat16)
-    sum_proj = Scatter(rows_product(activated, upstream_b).astype(jnp.bfloat16), False)
+
+    sum_proj = Scatter([rows_product(activated, upstream_b).astype(jnp.bfloat16)], True)
     out_proj = sum_proj.last()
     d_act = times_transposed(upstream_b, proj_weight)
     d_pre = gelu_back(pre_act, d_act)
     d_pre_b = d_pre.astype(jnp.bfloat16)
-    sum_fc = Scatter(rows_product(ln_two_b, d_pre_b).astype(jnp.bfloat16))
+    sum_fc = Scatter([rows_product(ln_two_b, d_pre_b).astype(jnp.bfloat16)])
     sum_fc.core()
     d_ln_two = times_transposed(d_pre_b, fc_weight)
     d_resid = upstream + norm_back(d_ln_two, gain_rows[1], normed_two, inv_two)
@@ -470,15 +470,14 @@
         )
     d_queries = jnp.concatenate([part[0] for part in own_parts], 0).reshape(row_count, width)
     query_sums = sum(part[1] for part in own_parts)
-    d_queries = gate(d_queries, sum_fc)
-    sum_fc.second()
     grad_query = rows_product(ln_one_b, d_queries).astype(jnp.bfloat16)
     grad_out = rows_product(attended, d_resid_b).astype(jnp.bfloat16)
-    sum_mid = Scatter(jnp.concatenate([grad_query, grad_out], 1))
+    sum_mid = Scatter([grad_query, grad_out], False, False)
     sum_mid.core()
-    arrived = gate(arrived, sum_fc, sum_mid)
+    arrived, final = gate((arrived, final), sum_fc, sum_mid)
+    block_out = (keep_rows * final).astype(jnp.bfloat16).reshape(slot_count, span, width)
+    sum_fc.second()
     sum_mid.first()
-    out_fc = sum_fc.last()
     own_terms = jnp.concatenate([part[2] for part in own_parts], 0) + jnp.concatenate(
         arrived, 0
     ).astype(jnp.float32)
@@ -488,7 +487,6 @@
         [d_queries, d_keys.astype(jnp.bfloat16), d_values_own.astype(jnp.bfloat16)], 1
     )
     d_ln_one = times_transposed(d_proj_in, qkv_weight)
-    sum_mid.second()
     grad_kv = rows_product(ln_one_b, d_proj_in[:, width:]).astype(jnp.bfloat16)
     d_input = d_resid + norm_back(d_ln_one, gain_rows[0], normed_one, inv_one)
     early = jnp.stack(
@@ -497,7 +495,7 @@
             jnp.sum(query_sums, (0, 1)),
             jnp.sum(d_resid, 0),
             jnp.sum(d_ln_two, 0),
-            jnp.sum(upstream, 0),
+            upstream_sum,
         ],
         0,
     )
@@ -507,8 +505,14 @@
     grad_shift = jnp.sum(d_pre, 0).reshape(width, per_col).T
     grad_small = jnp.concatenate([early, grad_shift, late], 0).T.astype(jnp.bfloat16)
     grad_small = jnp.pad(grad_small, ((0, 0), (0, PAD - SMALL)))
+    sum_last = Scatter([grad_kv, grad_small])
+    sum_last.core()
+    out_fc = sum_fc.last()
+    sum_mid.second()
+    sum_last.first()
     out_mid = sum_mid.last()
-    last = Scatter(jnp.concatenate([grad_kv, grad_small], 1)).all()
+    sum_last.second()
+    last = sum_last.last()
     out_out = out_mid[:, width:]
     out_qkv = jnp.concatenate([out_mid[:, :width], last[:, : 2 * width]], 1)
     own = last[:, 2 * width : 2 * width + SMALL].T

time: 389 us -> 363 us (0.933)
  Pallas kernels: 37.1 us -> 30.1 us
  starting transfers between devices: 46.7 us -> 40 us
  local copies, waits for them, and re-layouts: 55.8 us -> 51.1 us
    ppermute x33 -> x27, waiting for transfers between devices: 124 us -> 94.9 us  [move(): return lax.ppermute(block, BOTH, pairs)]
    ppermute x2, waiting for transfers between devices: 0.01 us -> 20 us  [on_device(): arrived.append(lax.ppermute(terms, BOTH, back))]
    ppermute x33 -> x27, starting transfers between devices: 41.1 us -> 32.7 us  [move(): return lax.ppermute(block, BOTH, pairs)]
    ppermute x2, waiting for transfers between devices: 16 us -> 23.3 us  [on_device(): before.append(lax.ppermute(block, BOTH, pairs))]
    pallas_call x2 -> x1, Pallas kernels: 12.9 us -> 6.41 us  [own_back(): pl.pallas_call(own_kernel, grid=(groups,), in_specs=[rows_spec(span, 0, s...]
    pallas_call x0 -> x1, local copies, waits for them, and re-layouts: none -> 6.31 us  [own_back(): pl.pallas_call(own_kernel, grid=(groups,), in_specs=[rows_spec(span, 0, s...]
    concatenate x1 -> x0, local copies, waits for them, and re-layouts: 4.42 us -> none  [on_device(): sum_mid = Scatter(jnp.concatenate([grad_query, grad_out], 1))]
    dot_general x1, matrix products: 9.15 us -> 5.21 us  [on_device(): jnp.dot(activated, proj_weight, preferred_element_type=jnp.float32)]
  transfers between devices with their start and end apart: 39 -> 33, of which waited for: 20 -> 19; matrix products, arithmetic and copies ran while one was open for 26% -> 22% of each run, Pallas kernels for 10% -> 3%
where the time goes in v1:
time: 363 us; the launch traced here: 357 us
  waiting for transfers between devices  138 us (38%)
  local copies, waits for them, and re-layouts  51.1 us (14%)
  matrix products  43.8 us (12%)
  starting transfers between devices  40 us (11%)
  other arithmetic  38 us (10%)
  Pallas kernels  30.1 us (8%)
  between operations  15.3 us (4%)
    ppermute x27, waiting for transfers between devices, move(): return lax.ppermute(block, BOTH, pairs)  94.9 us
    ppermute x27, starting transfers between devices, move(): return lax.ppermute(block, BOTH, pairs)  32.7 us
    ppermute x2, waiting for transfers between devices, on_device(): before.append(lax.ppermute(block, BOTH, pairs))  23.3 us
    ppermute x2, waiting for transfers between devices, on_device(): arrived.append(lax.ppermute(terms, BOTH, back))  20 us
    dot_general x5, matrix products, rows_product(): lax.dot_general(left, right, (((0,), (0,)), ((), ())), preferred_element_...  16.6 us
    dot_general x4, matrix products, times_transposed(): lax.dot_general(left, right, (((1,), (1,)), ((), ())), preferred_element_...  16.4 us
    unnamed x124, local copies, waits for them, and re-layouts  12.4 us
    pallas_call x2, Pallas kernels, far_back(): pl.pallas_call(far_kernel, grid_spec=pltpu.PrefetchScalarGridSpec(num_sca...  12.1 us
  transfers between devices with their start and end apart: 33, of which 19 were waited for; matrix products, arithmetic and copies ran while one was open for 22% of the time, Pallas kernels for 3%

profile of v1, /device:TPU:0, one launch (start us, length us, event | category | flops | bytes accessed | tf_op | source)
XLA Modules:
  0.0 356.7 jit_solution(8019584709006866019)
XLA Ops:
  15.0 7.8 %collective-permute-done.10 = bf16[216,768]{1,0:T(8,128)(2,1)S(1)} collective-permute-done((bf16[216,768]{1,0:T(8,128)(2,1)S(1)}, bf16[216,768]{1,0:T(8,128)(2,1)S(1)}, u32[]{:S(2)}, u32[]{:S(2)}) %collective-permute-start.10) | collective-permute-done | bytes 331808 | tf_op jit(solution)/shard_map/ppermute | solution.py:70
  39.3 8.8 %collective-permute-done.3 = bf16[4,24,1152]{2,1,0:T(8,128)(2,1)S(1)} collective-permute-done((bf16[4,24,1152]{2,1,0:T(8,128)(2,1)S(1)}, bf16[4,24,1152]{2,1,0:T(8,128)(2,1)S(1)}, u32[]{:S(2)}, u32[]{:S(2)}) %collective-permute-start.3) | collective-permute-done | bytes 221216 | tf_op jit(solution)/shard_map/ppermute | solution.py:70
  50.6 9.4 %collective-permute-done.4 = bf16[4,2,24,1152]{3,2,0,1:T(8,128)(2,1)S(1)} collective-permute-done((bf16[4,2,24,1152]{3,2,0,1:T(8,128)(2,1)S(1)}, bf16[4,2,24,1152]{3,2,0,1:T(8,128)(2,1)S(1)}, u32[]{:S(2)}, u32[]{:S(2)}) %collective-permute-start.4) | collective-permute-done | bytes 442400 | tf_op jit(solution)/shard_map/ppermute | solution.py:70
  65.4 4.9 %collective-permute-done.7 = bf16[4,2,2,24,2432]{4,3,2,1,0:T(8,128)(2,1)} collective-permute-done((bf16[4,2,2,24,2432]{4,3,2,1,0:T(8,128)(2,1)}, bf16[4,2,2,24,2432]{4,3,2,1,0:T(8,128)(2,1)}, u32[]{:S(2)}, u32[]{:S(2)}) %collective-permute-start.7) | collective-permute-done | bytes 1867808 | tf_op jit(solution)/shard_map/ppermute | solution.py:70
  92.9 23.3 %collective-permute-done.8.kf_ref.vf_ref.k_ref.v_ref = bf16[1,256,1536]{2,1,0:T(8,128)(2,1)S(1)} collective-permute-done((bf16[1,256,1536]{2,1,0:T(8,128)(2,1)}, bf16[1,256,1536]{2,1,0:T(8,128)(2,1)S(1)}, u32[]{:S(2)}, u32[]{:S(2)}) %collective-permute-start.8) | collective-permute-done | bytes 786464 | tf_op jit(solution)/shard_map/ppermute | solution.py:416
  117.2 5.9 %attend.2 = (bf16[1,256,768]{2,1,0:T(8,128)(2,1)}, f32[1,3,4,256]{3,2,1,0:T(4,128)}) custom-call(s32[1]{0:T(128)} %bitcast.limit, bf16[2,256,768]{2,1,0:T(8,128)(2,1)} %bitcast.230, bf16[2,256,1536]{2,1,0:T(8,128)(2,1)} %bitcast.223, bf16[2,256,1536]{2,1,0:T(8,128)(2,1)} %bitcast.224, bf16[1,256,1536]{2,1,0:T(8,128)(2,1)} %copy-done.6, ...), custom_call_target="tpu_custom_call" | custom-call | tf_op jit(solution)/shard_map/attend/pallas_call | solution.py:286
  124.0 5.8 %attend.3 = (bf16[1,256,768]{2,1,0:T(8,128)(2,1)}, f32[1,3,4,256]{3,2,1,0:T(4,128)}) custom-call(s32[1]{0:T(128)} %bitcast.limit, bf16[2,256,768]{2,1,0:T(8,128)(2,1)} %bitcast.231, bf16[2,256,1536]{2,1,0:T(8,128)(2,1)} %bitcast.225, bf16[2,256,1536]{2,1,0:T(8,128)(2,1)} %bitcast.226, bf16[1,256,1536]{2,1,0:T(8,128)(2,1)} %copy-done.5, ...), custom_call_target="tpu_custom_call" | custom-call | tf_op jit(solution)/shard_map/attend/pallas_call | solution.py:286
  138.7 4.9 %slice.206 = bf16[32,96,768]{2,1,0:T(8,128)(2,1)S(1)} slice(bf16[32,216,768]{2,1,0:T(8,128)(2,1)} %all-gather.2.cloned.1.call-done), slice={[0:32], [120:216], [0:768]} | slice | bytes 9437184 | tf_op jit(solution)/shard_map/slice | solution.py:397
  143.7 7.1 %fusion.83 = (bf16[3072]{0:T(1024)(128)(2,1)}, bf16[512,3072]{1,0:T(8,128)(2,1)S(1)}) fusion(f32[512,3072]{1,0:T(8,128)S(1)} %fusion.48, f32[3072]{0:T(1024)S(1)} %copy-done.40, bf16[512,768]{1,0:T(8,128)(2,1)S(1)} %copy-done.27, bf16[3072,768]{1,0:T(8,128)(2,1)S(1)} %bitcast.242), kind=kOutput, calls=%fused_computation.225 | convolution fusion | flops 2450519040 | bytes 14960640 | tf_op jit(solution)/shard_map/dot_general | solution.py:47
  164.5 5.2 %add_add_fusion = f32[512,768]{1,0:T(8,128)} fusion(f32[512,768]{1,0:T(8,128)S(1)} %get-tuple-element.184, bf16[3072,768]{1,0:T(8,128)(2,1)S(1)} %bitcast.243, f32[768]{0:T(1024)S(1)} %get-tuple-element.115, f32[512,3072]{1,0:T(8,128)S(1)} %fusion.48, f32[3072]{0:T(1024)S(1)} %copy-done.40), kind=kOutput, calls=%fused_computation.76 | convolution fusion | flops 2432434176 | bytes 14171136 | tf_op jit(solution)/shard_map/dot_general | solution.py:438
  172.0 5.9 %far_back.2 = (f32[1,256,768]{2,1,0:T(8,128)}, bf16[1,2,256,768]{3,2,1,0:T(8,128)(2,1)}) custom-call(s32[1]{0:T(128)} %bitcast.limit, bf16[2,256,768]{2,1,0:T(8,128)(2,1)} %bitcast.232, bf16[1,256,1536]{2,1,0:T(8,128)(2,1)} %copy-done.6, bf16[1,256,1536]{2,1,0:T(8,128)(2,1)} %copy-done.6, bf16[2,256,768]{2,1,0:T(8,128)(2,1)} %bitcast.236, ...), custom_call_target="tpu_custom_call" | custom-call | tf_op jit(solution)/shard_map/far_back/pallas_call | solution.py:311
  178.0 6.4 %own_back.2 = (bf16[1,256,768]{2,1,0:T(8,128)(2,1)}, f32[1,1,768]{2,1,0:T(1,128)}, f32[1,2,256,768]{3,2,1,0:T(8,128)}) custom-call(bf16[2,256,768]{2,1,0:T(8,128)(2,1)} %bitcast.233, bf16[2,256,1536]{2,1,0:T(8,128)(2,1)} %bitcast.227, bf16[2,256,1536]{2,1,0:T(8,128)(2,1)} %bitcast.228, bf16[2,256,768]{2,1,0:T(8,128)(2,1)} %bitcast.237, ...), custom_call_target="tpu_custom_call" | custom-call | tf_op jit(solution)/shard_map/own_back/pallas_call | solution.py:337
  186.1 6.1 %far_back.3 = (f32[1,256,768]{2,1,0:T(8,128)}, bf16[1,2,256,768]{3,2,1,0:T(8,128)(2,1)}) custom-call(s32[1]{0:T(128)} %bitcast.limit, bf16[2,256,768]{2,1,0:T(8,128)(2,1)} %bitcast.234, bf16[1,256,1536]{2,1,0:T(8,128)(2,1)} %copy-done.5, bf16[1,256,1536]{2,1,0:T(8,128)(2,1)} %copy-done.5, bf16[2,256,768]{2,1,0:T(8,128)(2,1)} %bitcast.238, ...), custom_call_target="tpu_custom_call" | custom-call | tf_op jit(solution)/shard_map/far_back/pallas_call | solution.py:311
  192.3 6.3 %own_back.3 = (bf16[2,256,768]{2,1,0:T(8,128)(2,1)}, f32[1,2,256,768]{3,2,1,0:T(8,128)}, f32[1,1,768]{2,1,0:T(1,128)}) fusion(bf16[2,256,768]{2,1,0:T(8,128)(2,1)} %constant_dynamic-update-slice_fusion.3, bf16[2,256,768]{2,1,0:T(8,128)(2,1)S(1)} %bitcast.235, bf16[2,256,1536]{2,1,0:T(8,128)(2,1)S(1)} %bitcast.229, bf16[2,256,768]{2,1,0:T(8,128)(2,1)} %bitcast.239, ...), kind=kCustom, calls=%fused_computation.191 | custom fusion | bytes 6306816 | tf_op jit(solution)/shard_map/own_back/pallas_call | solution.py:337
  205.1 8.7 %convolution_convert_fusion = bf16[3072,768]{1,0:T(8,128)(2,1)} fusion(bf16[512,768]{1,0:T(8,128)(2,1)S(1)} %copy-done.28, f32[512,3072]{1,0:T(8,128)} %copy-done.55, f32[3072]{0:T(1024)S(1)} %copy-done.41), kind=kOutput, calls=%fused_computation.9 | convolution fusion | flops 2434007040 | bytes 11808768 | tf_op jit(solution)/shard_map/dot_general | solution.py:41
  223.9 9.0 %collective-permute-done.14 = bf16[4,2,24,3072]{3,2,0,1:T(8,128)(2,1)} collective-permute-done((bf16[4,2,24,3072]{3,2,0,1:T(8,128)(2,1)}, bf16[4,2,24,3072]{3,2,0,1:T(8,128)(2,1)}, u32[]{:S(2)}, u32[]{:S(2)}) %collective-permute-start.14) | collective-permute-done | bytes 1179680 | tf_op jit(solution)/shard_map/ppermute | solution.py:70
  235.7 4.4 %collective-permute-done.12 = bf16[1,2,256,768]{3,2,1,0:T(8,128)(2,1)} collective-permute-done((bf16[1,2,256,768]{3,2,1,0:T(8,128)(2,1)}, bf16[1,2,256,768]{3,2,1,0:T(8,128)(2,1)}, u32[]{:S(2)}, u32[]{:S(2)}) %collective-permute-start.12) | collective-permute-done | bytes 786464 | tf_op jit(solution)/shard_map/ppermute | solution.py:463
  240.1 15.6 %collective-permute-done.13 = bf16[1,2,256,768]{3,2,1,0:T(8,128)(2,1)} collective-permute-done((bf16[1,2,256,768]{3,2,1,0:T(8,128)(2,1)}, bf16[1,2,256,768]{3,2,1,0:T(8,128)(2,1)}, u32[]{:S(2)}, u32[]{:S(2)}) %collective-permute-start.13) | collective-permute-done | bytes 786464 | tf_op jit(solution)/shard_map/ppermute | solution.py:463
  262.5 4.0 %fusion.39 = (bf16[768]{0:T(1024)(128)(2,1)S(1)}, f32[512]{0:T(512)S(1)}, f32[512]{0:T(512)}, bf16[768]{0:T(1024)(128)(2,1)S(1)}, f32[512,768]{1,0:T(8,128)}) fusion(bf16[2,256,768]{2,1,0:T(8,128)(2,1)S(1)} %copy-done.4, f32[512]{0:T(512)S(1)} %bitcast.282, f32[512]{0:T(512)S(1)} %bitcast.279, f32[768]{0:T(1024)S(1)} %get-tuple-element.119, ...), kind=kOutput, calls=%fused_computation.72 | convolution fusion | flops 1822946816 | bytes 8272896 | tf_op jit(solution)/shard_map/dot_general | solution.py:47
  279.1 12.2 %collective-permute-done.27 = bf16[4,24,3072]{2,1,0:T(8,128)(2,1)S(1)} collective-permute-done((bf16[4,24,3072]{2,1,0:T(8,128)(2,1)S(1)}, bf16[4,24,3072]{2,1,0:T(8,128)(2,1)S(1)}, u32[]{:S(2)}, u32[]{:S(2)}) %collective-permute-start.27) | collective-permute-done | bytes 589856 | tf_op jit(solution)/shard_map/ppermute | solution.py:70
  295.8 8.0 %collective-permute-done.22 = bf16[4,2,24,1536]{3,2,1,0:T(8,128)(2,1)S(1)} collective-permute-done((bf16[4,2,24,1536]{3,2,1,0:T(8,128)(2,1)S(1)}, bf16[4,2,24,1536]{3,2,1,0:T(8,128)(2,1)S(1)}, u32[]{:S(2)}, u32[]{:S(2)}) %collective-permute-start.22) | collective-permute-done | bytes 589856 | tf_op jit(solution)/shard_map/ppermute | solution.py:70
  305.8 4.9 %collective-permute-done.29 = bf16[24,3072]{1,0:T(8,128)(2,1)S(1)} collective-permute-done((bf16[24,3072]{1,0:T(8,128)(2,1)S(1)}, bf16[24,3072]{1,0:T(8,128)(2,1)S(1)}, u32[]{:S(2)}, u32[]{:S(2)}) %collective-permute-start.29) | collective-permute-done | bytes 147488 | tf_op jit(solution)/shard_map/ppermute | solution.py:70
  317.4 10.4 %collective-permute-done.17 = bf16[4,2,24,1664]{3,2,1,0:T(8,128)(2,1)S(1)} collective-permute-done((bf16[4,2,24,1664]{3,2,1,0:T(8,128)(2,1)S(1)}, bf16[4,2,24,1664]{3,2,1,0:T(8,128)(2,1)S(1)}, u32[]{:S(2)}, u32[]{:S(2)}) %collective-permute-start.17) | collective-permute-done | bytes 639008 | tf_op jit(solution)/shard_map/ppermute | solution.py:70
  328.8 6.5 %collective-permute-done.18 = bf16[4,24,1664]{2,1,0:T(8,128)(2,1)S(1)} collective-permute-done((bf16[4,24,1664]{2,1,0:T(8,128)(2,1)S(1)}, bf16[4,24,1664]{2,1,0:T(8,128)(2,1)S(1)}, u32[]{:S(2)}, u32[]{:S(2)}) %collective-permute-start.18) | collective-permute-done | bytes 319520 | tf_op jit(solution)/shard_map/ppermute | solution.py:70
  (299 shorter events, 149.7 us)
Async XLA Ops:
  7.2 124.4 %all-gather.2.cloned.1.call-start = ((), (), s32[]{:S(2)}) async-start(), calls=%async_computation.1 | async-start | bytes 11280384 | tf_op jit(solution)/shard_map/all_gather | solution.py:381
  12.0 10.8 %collective-permute-start.10 = (bf16[216,768]{1,0:T(8,128)(2,1)S(1)}, bf16[216,768]{1,0:T(8,128)(2,1)S(1)}, u32[]{:S(2)}, u32[]{:S(2)}) collective-permute-start(bf16[216,768]{1,0:T(8,128)(2,1)S(1)} %constant_dynamic-update-slice_fusion), channel_id=1, source_target_pairs={{0,1},{1,0},{2,3},{3,2},{4,5},{5,4},{6,7},{7,6},{8,9},{9,8},{10,11... | collective-permute-start | bytes 995336 | tf_op jit(solution)/shard_map/ppermute | solution.py:70
  23.8 324.1 %reduce-scatter.2.cloned.1.call-start = ((), (), s32[]{:S(2)}) async-start(), calls=%async_computation.2 | async-start | bytes 4866048 | tf_op jit(solution)/shard_map/reduce_scatter | solution.py:150
  36.2 12.0 %collective-permute-start.3 = (bf16[4,24,1152]{2,1,0:T(8,128)(2,1)S(1)}, bf16[4,24,1152]{2,1,0:T(8,128)(2,1)S(1)}, u32[]{:S(2)}, u32[]{:S(2)}) collective-permute-start(bf16[4,24,1152]{2,1,0:T(8,128)(2,1)S(1)} %pad_maximum_fusion.15), channel_id=1, source_target_pairs={{0,4},{1,5},{2,6},{3,7},{4,0},{5,1},{6,2},{7,3},{8,12},{9,13},{10,... | collective-permute-start | bytes 663560 | tf_op jit(solution)/shard_map/ppermute | solution.py:70
  37.8 12.1 %collective-permute-start.5 = (bf16[4,24,1280]{2,1,0:T(8,128)(2,1)S(1)}, bf16[4,24,1280]{2,1,0:T(8,128)(2,1)S(1)}, u32[]{:S(2)}, u32[]{:S(2)}) collective-permute-start(bf16[4,24,1280]{2,1,0:T(8,128)(2,1)S(1)} %pad_maximum_fusion.12), channel_id=1, source_target_pairs={{0,1},{1,0},{2,3},{3,2},{4,5},{5,4},{6,7},{7,6},{8,9},{9,8},{10,11... | collective-permute-start | bytes 737288 | tf_op jit(solution)/shard_map/ppermute | solution.py:70
  48.3 11.7 %collective-permute-start.4 = (bf16[4,2,24,1152]{3,2,0,1:T(8,128)(2,1)S(1)}, bf16[4,2,24,1152]{3,2,0,1:T(8,128)(2,1)S(1)}, u32[]{:S(2)}, u32[]{:S(2)}) collective-permute-start(bf16[4,2,24,1152]{3,2,0,1:T(8,128)(2,1)S(1)} %pad_maximum_fusion.11), channel_id=1, source_target_pairs={{0,1},{1,0},{2,3},{3,2},{4,5},{5,4},{6,7},{7,6},{8,9},{9,8},{10,11... | collective-permute-start | bytes 1327112 | tf_op jit(solution)/shard_map/ppermute | solution.py:70
  50.0 12.6 %collective-permute-start.6 = (bf16[4,2,24,1280]{3,2,1,0:T(8,128)(2,1)S(1)}, bf16[4,2,24,1280]{3,2,1,0:T(8,128)(2,1)S(1)}, u32[]{:S(2)}, u32[]{:S(2)}) collective-permute-start(bf16[4,2,24,1280]{3,2,1,0:T(8,128)(2,1)S(1)} %pad_maximum_fusion.10), channel_id=1, source_target_pairs={{0,4},{1,5},{2,6},{3,7},{4,0},{5,1},{6,2},{7,3},{8,12},{9,13},{10,... | collective-permute-start | bytes 1474568 | tf_op jit(solution)/shard_map/ppermute | solution.py:70
  79.2 43.9 %collective-permute-start.9 = (bf16[1,256,1536]{2,1,0:T(8,128)(2,1)}, bf16[1,256,1536]{2,1,0:T(8,128)(2,1)S(1)}, u32[]{:S(2)}, u32[]{:S(2)}) collective-permute-start(bf16[1,256,1536]{2,1,0:T(8,128)(2,1)} %get-tuple-element.142), channel_id=1, source_target_pairs={{0,1},{2,3},{4,5},{6,7},{8,9},{10,11},{12,13},{14,15},{16,17},{18,... | collective-permute-start | bytes 2359304 | tf_op jit(solution)/shard_map/ppermute | solution.py:416
  82.0 34.2 %collective-permute-start.8 = (bf16[1,256,1536]{2,1,0:T(8,128)(2,1)}, bf16[1,256,1536]{2,1,0:T(8,128)(2,1)S(1)}, u32[]{:S(2)}, u32[]{:S(2)}) collective-permute-start(bf16[1,256,1536]{2,1,0:T(8,128)(2,1)} %get-tuple-element.143), channel_id=1, source_target_pairs={{0,1},{2,3},{4,5},{6,7},{8,9},{10,11},{12,13},{14,15},{16,17},{18,... | collective-permute-start | bytes 2359304 | tf_op jit(solution)/shard_map/ppermute | solution.py:416
  158.6 11.2 %collective-permute-start.11 = (bf16[4,2,2,24,3072]{4,3,0,2,1:T(8,128)(2,1)S(1)}, bf16[4,2,2,24,3072]{4,3,0,2,1:T(8,128)(2,1)S(1)}, u32[]{:S(2)}, u32[]{:S(2)}) collective-permute-start(bf16[4,2,2,24,3072]{4,3,0,2,1:T(8,128)(2,1)S(1)} %bitcast.251), channel_id=1, source_target_pairs={{0,2},{1,3},{2,0},{3,1},{4,6},{5,7},{6,4},{7,5},{8,10},{9,11},{10,... | collective-permute-start | bytes 7077896 | tf_op jit(solution)/shard_map/ppermute | solution.py:70
  203.1 17.8 %collective-permute-start.15 = (bf16[4,2,2,24,1536]{4,3,2,1,0:T(8,128)(2,1)}, bf16[4,2,2,24,1536]{4,3,2,1,0:T(8,128)(2,1)}, u32[]{:S(2)}, u32[]{:S(2)}) collective-permute-start(bf16[4,2,2,24,1536]{4,3,2,1,0:T(8,128)(2,1)} %pad_maximum_fusion.4), channel_id=1, source_target_pairs={{0,2},{1,3},{2,0},{3,1},{4,6},{5,7},{6,4},{7,5},{8,10},{9,11},{10,... | collective-permute-start | bytes 3538952 | tf_op jit(solution)/shard_map/ppermute | solution.py:70
  205.0 28.0 %collective-permute-start.14 = (bf16[4,2,24,3072]{3,2,0,1:T(8,128)(2,1)}, bf16[4,2,24,3072]{3,2,0,1:T(8,128)(2,1)}, u32[]{:S(2)}, u32[]{:S(2)}) collective-permute-start(bf16[4,2,24,3072]{3,2,0,1:T(8,128)(2,1)} %dynamic-slice_bitcast_fusion.2), channel_id=1, source_target_pairs={{0,4},{1,5},{2,6},{3,7},{4,0},{5,1},{6,2},{7,3},{8,12},{9,13},{10,... | collective-permute-start | bytes 3538952 | tf_op jit(solution)/shard_map/ppermute | solution.py:70
  217.5 22.6 %collective-permute-start.12 = (bf16[1,2,256,768]{3,2,1,0:T(8,128)(2,1)}, bf16[1,2,256,768]{3,2,1,0:T(8,128)(2,1)}, u32[]{:S(2)}, u32[]{:S(2)}) collective-permute-start(bf16[1,2,256,768]{3,2,1,0:T(8,128)(2,1)} %get-tuple-element.47), channel_id=1, source_target_pairs={{1,0},{3,2},{5,4},{7,6},{9,8},{11,10},{13,12},{15,14},{17,16},{19,... | collective-permute-start | bytes 2359304 | tf_op jit(solution)/shard_map/ppermute | solution.py:463
  218.8 36.9 %collective-permute-start.13 = (bf16[1,2,256,768]{3,2,1,0:T(8,128)(2,1)}, bf16[1,2,256,768]{3,2,1,0:T(8,128)(2,1)}, u32[]{:S(2)}, u32[]{:S(2)}) collective-permute-start(bf16[1,2,256,768]{3,2,1,0:T(8,128)(2,1)} %get-tuple-element.49), channel_id=1, source_target_pairs={{1,0},{3,2},{5,4},{7,6},{9,8},{11,10},{13,12},{15,14},{17,16},{19,... | collective-permute-start | bytes 2359304 | tf_op jit(solution)/shard_map/ppermute | solution.py:463
  275.0 16.3 %collective-permute-start.27 = (bf16[4,24,3072]{2,1,0:T(8,128)(2,1)S(1)}, bf16[4,24,3072]{2,1,0:T(8,128)(2,1)S(1)}, u32[]{:S(2)}, u32[]{:S(2)}) collective-permute-start(bf16[4,24,3072]{2,1,0:T(8,128)(2,1)S(1)} %dynamic-slice_bitcast_fusion.4), channel_id=1, source_target_pairs={{0,1},{1,0},{2,3},{3,2},{4,5},{5,4},{6,7},{7,6},{8,9},{9,8},{10,11... | collective-permute-start | bytes 1769480 | tf_op jit(solution)/shard_map/ppermute | solution.py:70
  275.1 28.8 %collective-permute-start.22 = (bf16[4,2,24,1536]{3,2,1,0:T(8,128)(2,1)S(1)}, bf16[4,2,24,1536]{3,2,1,0:T(8,128)(2,1)S(1)}, u32[]{:S(2)}, u32[]{:S(2)}) collective-permute-start(bf16[4,2,24,1536]{3,2,1,0:T(8,128)(2,1)S(1)} %dynamic-slice_bitcast_fusion.5), channel_id=1, source_target_pairs={{0,1},{1,0},{2,3},{3,2},{4,5},{5,4},{6,7},{7,6},{8,9},{9,8},{10,11... | collective-permute-start | bytes 1769480 | tf_op jit(solution)/shard_map/ppermute | solution.py:70
  277.2 34.2 %collective-permute-start.16 = (bf16[4,2,2,24,1664]{4,3,2,1,0:T(8,128)(2,1)S(1)}, bf16[4,2,2,24,1664]{4,3,2,1,0:T(8,128)(2,1)S(1)}, u32[]{:S(2)}, u32[]{:S(2)}) collective-permute-start(bf16[4,2,2,24,1664]{4,3,2,1,0:T(8,128)(2,1)S(1)} %pad_maximum_fusion.3), channel_id=1, source_target_pairs={{0,2},{1,3},{2,0},{3,1},{4,6},{5,7},{6,4},{7,5},{8,10},{9,11},{10,... | collective-permute-start | bytes 3833864 | tf_op jit(solution)/shard_map/ppermute | solution.py:70
  291.5 14.3 %collective-permute-start.28 = (bf16[24,3072]{1,0:T(8,128)(2,1)S(1)}, bf16[24,3072]{1,0:T(8,128)(2,1)S(1)}, u32[]{:S(2)}, u32[]{:S(2)}) collective-permute-start(bf16[24,3072]{1,0:T(8,128)(2,1)S(1)} %get-tuple-element.154), channel_id=1, source_target_pairs={{0,8},{1,9},{2,10},{3,11},{4,12},{5,13},{6,14},{7,15},{8,16},{9,17... | collective-permute-start | bytes 442376 | tf_op jit(solution)/shard_map/ppermute | solution.py:70
  292.7 13.0 %collective-permute-start.30 = (bf16[24,3072]{1,0:T(8,128)(2,1)S(1)}, bf16[24,3072]{1,0:T(8,128)(2,1)S(1)}, u32[]{:S(2)}, u32[]{:S(2)}) collective-permute-start(bf16[24,3072]{1,0:T(8,128)(2,1)S(1)} %get-tuple-element.155), channel_id=1, source_target_pairs={{0,24},{1,25},{2,26},{3,27},{4,28},{5,29},{6,30},{7,31},{8,0},{9,1... | collective-permute-start | bytes 442376 | tf_op jit(solution)/shard_map/ppermute | solution.py:70
  295.4 15.3 %collective-permute-start.29 = (bf16[24,3072]{1,0:T(8,128)(2,1)S(1)}, bf16[24,3072]{1,0:T(8,128)(2,1)S(1)}, u32[]{:S(2)}, u32[]{:S(2)}) collective-permute-start(bf16[24,3072]{1,0:T(8,128)(2,1)S(1)} %get-tuple-element.156), channel_id=1, source_target_pairs={{0,16},{1,17},{2,18},{3,19},{4,20},{5,21},{6,22},{7,23},{8,24},{9,... | collective-permute-start | bytes 442376 | tf_op jit(solution)/shard_map/ppermute | solution.py:70
  311.8 16.0 %collective-permute-start.17 = (bf16[4,2,24,1664]{3,2,1,0:T(8,128)(2,1)S(1)}, bf16[4,2,24,1664]{3,2,1,0:T(8,128)(2,1)S(1)}, u32[]{:S(2)}, u32[]{:S(2)}) collective-permute-start(bf16[4,2,24,1664]{3,2,1,0:T(8,128)(2,1)S(1)} %dynamic-slice_bitcast_fusion.3), channel_id=1, source_target_pairs={{0,4},{1,5},{2,6},{3,7},{4,0},{5,1},{6,2},{7,3},{8,12},{9,13},{10,... | collective-permute-start | bytes 1916936 | tf_op jit(solution)/shard_map/ppermute | solution.py:70
  313.5 15.2 %collective-permute-start.24 = (bf16[24,1536]{1,0:T(8,128)(2,1)S(1)}, bf16[24,1536]{1,0:T(8,128)(2,1)S(1)}, u32[]{:S(2)}, u32[]{:S(2)}) collective-permute-start(bf16[24,1536]{1,0:T(8,128)(2,1)S(1)} %get-tuple-element.167), channel_id=1, source_target_pairs={{0,8},{1,9},{2,10},{3,11},{4,12},{5,13},{6,14},{7,15},{8,16},{9,17... | collective-permute-start | bytes 221192 | tf_op jit(solution)/shard_map/ppermute | solution.py:70
  313.8 14.9 %collective-permute-start.26 = (bf16[24,1536]{1,0:T(8,128)(2,1)S(1)}, bf16[24,1536]{1,0:T(8,128)(2,1)S(1)}, u32[]{:S(2)}, u32[]{:S(2)}) collective-permute-start(bf16[24,1536]{1,0:T(8,128)(2,1)S(1)} %get-tuple-element.168), channel_id=1, source_target_pairs={{0,24},{1,25},{2,26},{3,27},{4,28},{5,29},{6,30},{7,31},{8,0},{9,1... | collective-permute-start | bytes 221192 | tf_op jit(solution)/shard_map/ppermute | solution.py:70
  317.4 11.4 %collective-permute-start.25 = (bf16[24,1536]{1,0:T(8,128)(2,1)S(1)}, bf16[24,1536]{1,0:T(8,128)(2,1)S(1)}, u32[]{:S(2)}, u32[]{:S(2)}) collective-permute-start(bf16[24,1536]{1,0:T(8,128)(2,1)S(1)} %get-tuple-element.169), channel_id=1, source_target_pairs={{0,16},{1,17},{2,18},{3,19},{4,20},{5,21},{6,22},{7,23},{8,24},{9,... | collective-permute-start | bytes 221192 | tf_op jit(solution)/shard_map/ppermute | solution.py:70
  (65 other events, 444.6 us)
Sparse Core Ops, SparseCore 0:
  24.0 90.5 all-gather.1
  214.0 113.9 reduce-scatter.1

commit v2 on v1

--- a/solution.py
+++ b/solution.py
@@ -107,18 +107,14 @@
 
 
 def summed(mine, arrived):
-    return (mine.astype(jnp.float32) + arrived.astype(jnp.float32)).astype(jnp.bfloat16)
-
-
-def added(block, at, axis, arrived):
-    return summed(taken(block, at, axis), arrived)
+    return mine.astype(jnp.float32) + arrived.astype(jnp.float32)
 
 
 class Scatter:
-    def __init__(self, pieces, flat=False, y_first=True):
+    def __init__(self, pieces, flat=False):
         devices = lax.axis_size("dp") * lax.axis_size("ctx")
         self.grid = on_grid() and not flat
-        self.y_first = y_first
+        self.left = ["z", "y", "x"]
         lead = GRID if self.grid else (devices,)
         self.held = [
             piece.reshape(lead + (piece.shape[0] // devices, piece.shape[1])) for piece in pieces
@@ -129,33 +125,40 @@
             c = place()[2]
             sent = jnp.concatenate([taken(piece, 1 - c, 2) for piece in self.held], -1)
             mine = jnp.concatenate([taken(piece, c, 2) for piece in self.held], -1)
-            self.held = summed(mine, move(sent, 2, 1))
-
-    def pair(self, axis, at, dim):
-        self.held = added(self.held, at, dim, move(taken(self.held, 1 - at, dim), axis, 1))
-
-    def first(self):
+            self.held = summed(mine, move(sent, 2, 1)).astype(jnp.bfloat16)
+
+    def stage(self, name):
+        if not self.grid:
+            return
+        z, y, _, x = place()
+        axis, at, size = {"z": (0, z, 4), "y": (1, y, 2), "x": (3, x, 2)}[name]
+        dim = self.left.index(name)
+        self.left.remove(name)
+        total = taken(self.held, at, dim)
+        for step in range(1, size):
+            total = summed(total, move(taken(self.held, (at + step) % size, dim), axis, step))
+        self.held = total.astype(jnp.bfloat16) if self.left else total
+
+    def halves(self):
+        cut = self.held.shape[-1] // 256 * 128 if self.grid else 0
+        parts = []
+        for part in (slice(0, cut), slice(cut, None)):
+            half = Scatter([])
+            half.grid, half.left = self.grid, list(self.left)
+            half.held = self.held[..., part] if self.grid else None
+            parts.append(half)
+        return parts
+
+    def join(self, parts):
         if self.grid:
-            _, y, _, x = place()
-            self.pair(*((1, y, 1) if self.y_first else (3, x, 2)))
-
-    def second(self):
+            self.left = list(parts[0].left)
+            self.held = jnp.concatenate([part.held for part in parts], -1)
+
+    def result(self):
         if self.grid:
-            _, y, _, x = place()
-            self.pair(*((3, x, 1) if self.y_first else (1, y, 1)))
-
-    def last(self):
-        if not self.grid:
-            whole = jnp.concatenate(self.held, -1)
-            return lax.psum_scatter(whole, BOTH, scatter_dimension=0, tiled=False).astype(
-                jnp.float32
-            )
-        z = place()[0]
-        total = taken(self.held, z, 0).astype(jnp.float32)
-        for step in (1, 2, 3):
-            sent = taken(self.held, (z + step) % 4, 0)
-            total = total + move(sent, 0, step).astype(jnp.float32)
-        return total
+            return self.held
+        whole = jnp.concatenate(self.held, -1)
+        return lax.psum_scatter(whole, BOTH, scatter_dimension=0, tiled=False).astype(jnp.float32)
 
 
 def gate(value, *scatters):
@@ -404,13 +407,15 @@
     queries = (projected[:, :width] + bias_rows[1]).astype(jnp.bfloat16)
     keys_local = projected[:, width : 2 * width].astype(jnp.bfloat16)
     values_local = (projected[:, 2 * width :] + bias_rows[2]).astype(jnp.bfloat16)
-    key_value = jnp.concatenate([keys_local, values_local], 1).reshape(slot_count, span, 2 * width)
+    key_value = jnp.concatenate([keys_local, values_local], 1)
+    key_value = key_value.reshape(slot_count, span, 2 * width)
     rank = lax.axis_index("ctx")
     limit = (rank * span).reshape(1).astype(jnp.int32)
     queries = queries.reshape(slot_count, span, width)
     before, attended_list, logs = [], [], []
     for slot in range(slot_count):
-        block = key_value[slot : slot + 1]
+        rows = slice(slot * span, (slot + 1) * span)
+        block = jnp.concatenate([keys_local[rows], values_local[rows]], 1)[None]
         if paired:
             pairs = [(2 * i, 2 * i + 1) for i in range(devices // 2)]
             before.append(lax.ppermute(block, BOTH, pairs))
@@ -418,7 +423,8 @@
             before.append(lax.all_gather(block, "ctx", axis=1, tiled=True))
     upstream = keep_rows * cotangent.reshape(row_count, width).astype(jnp.float32)
     upstream_b = upstream.astype(jnp.bfloat16)
-    waited = (before[0], key_value, queries, fc_shift, upstream_b, bias_rows, jnp.sum(upstream, 0))
+    upstream_sum = jnp.sum(upstream, 0)
+    waited = (before[0], key_value, queries, fc_shift, upstream_b, bias_rows, upstream_sum)
     waited = lax.optimization_barrier(waited)
     before[0], key_value, queries, fc_shift, upstream_b, bias_rows, upstream_sum = waited
     for slot in range(slot_count):
@@ -440,7 +446,7 @@
     )
 
     sum_proj = Scatter([rows_product(activated, upstream_b).astype(jnp.bfloat16)], True)
-    out_proj = sum_proj.last()
+    out_proj = sum_proj.result()
     d_act = times_transposed(upstream_b, proj_weight)
     d_pre = gelu_back(pre_act, d_act)
     d_pre_b = d_pre.astype(jnp.bfloat16)
@@ -451,7 +457,7 @@
     d_resid_b = d_resid.astype(jnp.bfloat16)
     d_att = times_transposed(d_resid_b, out_weight).astype(jnp.bfloat16)
     d_att = gate(d_att, sum_fc).reshape(slot_count, span, width)
-    sum_fc.first()
+    sum_fc.stage("y")
     d_far, arrived = [], []
     for slot in range(slot_count):
         d_part, terms = far_back(
@@ -472,15 +478,17 @@
     query_sums = sum(part[1] for part in own_parts)
     grad_query = rows_product(ln_one_b, d_queries).astype(jnp.bfloat16)
     grad_out = rows_product(attended, d_resid_b).astype(jnp.bfloat16)
-    sum_mid = Scatter([grad_query, grad_out], False, False)
+    sum_mid = Scatter([grad_query, grad_out])
     sum_mid.core()
     arrived, final = gate((arrived, final), sum_fc, sum_mid)
+    sum_mid.stage("y")
+    sum_fc.stage("z")
     block_out = (keep_rows * final).astype(jnp.bfloat16).reshape(slot_count, span, width)
-    sum_fc.second()
-    sum_mid.first()
     own_terms = jnp.concatenate([part[2] for part in own_parts], 0) + jnp.concatenate(
         arrived, 0
     ).astype(jnp.float32)
+    sum_mid.stage("x")
+    sum_fc.stage("x")
     d_keys = own_terms[:, 0].reshape(row_count, width)
     d_values_own = own_terms[:, 1].reshape(row_count, width)
     d_proj_in = jnp.concatenate(
@@ -507,12 +515,15 @@
     grad_small = jnp.pad(grad_small, ((0, 0), (0, PAD - SMALL)))
     sum_last = Scatter([grad_kv, grad_small])
     sum_last.core()
-    out_fc = sum_fc.last()
-    sum_mid.second()
-    sum_last.first()
-    out_mid = sum_mid.last()
-    sum_last.second()
-    last = sum_last.last()
+    sum_mid.stage("z")
+    parts = sum_last.halves()
+    parts[0].stage("x")
+    parts[1].stage("y")
+    parts[0].stage("y")
+    parts[1].stage("x")
+    sum_last.join(parts)
+    sum_last.stage("z")
+    out_fc, out_mid, last = sum_fc.result(), sum_mid.result(), sum_last.result()
     out_out = out_mid[:, width:]
     out_qkv = jnp.concatenate([out_mid[:, :width], last[:, : 2 * width]], 1)
     own = last[:, 2 * width : 2 * width + SMALL].T

time: 363 us -> 373 us (1.028)
  waiting for transfers between devices: 138 us -> 143 us
    ppermute x27 -> x29, waiting for transfers between devices: 94.9 us -> 110 us  [move(): return lax.ppermute(block, BOTH, pairs)]
    ppermute x2, waiting for transfers between devices: 23.3 us -> 13.4 us  [on_device(): before.append(lax.ppermute(block, BOTH, pairs))]
    ppermute x27 -> x29, starting transfers between devices: 32.7 us -> 34 us  [move(): return lax.ppermute(block, BOTH, pairs)]
    convert_element_type x10 -> x12, other arithmetic: 10.6 us -> 10.6 us  [the longest x3 5.57 us: core(): self.held = summed(mine, move(sent, 2, 1)).astype(jnp.bfloat16)]
  transfers between devices with their start and end apart: 33 -> 35, of which waited for: 19 -> 26; matrix products, arithmetic and copies ran while one was open for 22% -> 22% of each run, Pallas kernels for 3% -> 3%
where the time goes in v2:
time: 373 us; the launch traced here: 366 us
  waiting for transfers between devices  143 us (38%)
  local copies, waits for them, and re-layouts  52.9 us (14%)
  matrix products  43.3 us (12%)
  starting transfers between devices  41.3 us (11%)
  other arithmetic  39.5 us (11%)
  Pallas kernels  30.2 us (8%)
  between operations  15.4 us (4%)
    ppermute x29, waiting for transfers between devices, move(): return lax.ppermute(block, BOTH, pairs)  110 us
    ppermute x29, starting transfers between devices, move(): return lax.ppermute(block, BOTH, pairs)  34 us
    ppermute x2, waiting for transfers between devices, on_device(): arrived.append(lax.ppermute(terms, BOTH, back))  19.9 us
    dot_general x5, matrix products, rows_product(): lax.dot_general(left, right, (((0,), (0,)), ((), ())), preferred_element_...  16.6 us
    dot_general x4, matrix products, times_transposed(): lax.dot_general(left, right, (((1,), (1,)), ((), ())), preferred_element_...  15.8 us
    ppermute x2, waiting for transfers between devices, on_device(): before.append(lax.ppermute(block, BOTH, pairs))  13.4 us
    pallas_call x2, Pallas kernels, far_back(): pl.pallas_call(far_kernel, grid_spec=pltpu.PrefetchScalarGridSpec(num_sca...  12.2 us
    unnamed x124, local copies, waits for them, and re-layouts  11.9 us
  transfers between devices with their start and end apart: 35, of which 26 were waited for; matrix products, arithmetic and copies ran while one was open for 22% of the time, Pallas kernels for 3%

profile of v2, /device:TPU:0, one launch (start us, length us, event | category | flops | bytes accessed | tf_op | source)
XLA Modules:
  0.0 365.9 jit_solution(12407979772076953128)
XLA Ops:
  15.0 7.8 %collective-permute-done.10 = bf16[216,768]{1,0:T(8,128)(2,1)S(1)} collective-permute-done((bf16[216,768]{1,0:T(8,128)(2,1)S(1)}, bf16[216,768]{1,0:T(8,128)(2,1)S(1)}, u32[]{:S(2)}, u32[]{:S(2)}) %collective-permute-start.10) | collective-permute-done | bytes 331808 | tf_op jit(solution)/shard_map/ppermute | solution.py:70
  39.3 8.8 %collective-permute-done.3 = bf16[4,24,1152]{2,1,0:T(8,128)(2,1)S(1)} collective-permute-done((bf16[4,24,1152]{2,1,0:T(8,128)(2,1)S(1)}, bf16[4,24,1152]{2,1,0:T(8,128)(2,1)S(1)}, u32[]{:S(2)}, u32[]{:S(2)}) %collective-permute-start.3) | collective-permute-done | bytes 221216 | tf_op jit(solution)/shard_map/ppermute | solution.py:70
  50.6 9.4 %collective-permute-done.4 = bf16[4,2,24,1152]{3,2,0,1:T(8,128)(2,1)S(1)} collective-permute-done((bf16[4,2,24,1152]{3,2,0,1:T(8,128)(2,1)S(1)}, bf16[4,2,24,1152]{3,2,0,1:T(8,128)(2,1)S(1)}, u32[]{:S(2)}, u32[]{:S(2)}) %collective-permute-start.4) | collective-permute-done | bytes 442400 | tf_op jit(solution)/shard_map/ppermute | solution.py:70
  65.4 4.9 %collective-permute-done.7 = bf16[4,2,2,24,2432]{4,3,2,1,0:T(8,128)(2,1)} collective-permute-done((bf16[4,2,2,24,2432]{4,3,2,1,0:T(8,128)(2,1)}, bf16[4,2,2,24,2432]{4,3,2,1,0:T(8,128)(2,1)}, u32[]{:S(2)}, u32[]{:S(2)}) %collective-permute-start.7) | collective-permute-done | bytes 1867808 | tf_op jit(solution)/shard_map/ppermute | solution.py:70
  96.2 4.2 %collective-permute-done.8.kf_ref.vf_ref.k_ref.v_ref = bf16[1,256,1536]{2,1,0:T(8,128)(2,1)S(1)} collective-permute-done((bf16[1,256,1536]{2,1,0:T(8,128)(2,1)}, bf16[1,256,1536]{2,1,0:T(8,128)(2,1)S(1)}, u32[]{:S(2)}, u32[]{:S(2)}) %collective-permute-start.8) | collective-permute-done | bytes 786464 | tf_op jit(solution)/shard_map/ppermute | solution.py:421
  101.5 5.8 %attend.2 = (bf16[1,256,768]{2,1,0:T(8,128)(2,1)}, f32[1,3,4,256]{3,2,1,0:T(4,128)}) custom-call(s32[1]{0:T(128)} %bitcast.limit, bf16[2,256,768]{2,1,0:T(8,128)(2,1)} %bitcast.242, bf16[2,256,1536]{2,1,0:T(8,128)(2,1)} %bitcast.235, bf16[2,256,1536]{2,1,0:T(8,128)(2,1)} %bitcast.236, bf16[1,256,1536]{2,1,0:T(8,128)(2,1)} %copy-done.8, ...), custom_call_target="tpu_custom_call" | custom-call | tf_op jit(solution)/shard_map/attend/pallas_call | solution.py:289
  107.3 9.2 %collective-permute-done.9.kf_ref.vf_ref.k_ref.v_ref = bf16[1,256,1536]{2,1,0:T(8,128)(2,1)S(1)} collective-permute-done((bf16[1,256,1536]{2,1,0:T(8,128)(2,1)}, bf16[1,256,1536]{2,1,0:T(8,128)(2,1)S(1)}, u32[]{:S(2)}, u32[]{:S(2)}) %collective-permute-start.9) | collective-permute-done | bytes 786464 | tf_op jit(solution)/shard_map/ppermute | solution.py:421
  117.4 5.8 %attend.3 = (bf16[1,256,768]{2,1,0:T(8,128)(2,1)}, f32[1,3,4,256]{3,2,1,0:T(4,128)}) custom-call(s32[1]{0:T(128)} %bitcast.limit, bf16[2,256,768]{2,1,0:T(8,128)(2,1)} %bitcast.243, bf16[2,256,1536]{2,1,0:T(8,128)(2,1)} %bitcast.237, bf16[2,256,1536]{2,1,0:T(8,128)(2,1)} %bitcast.238, bf16[1,256,1536]{2,1,0:T(8,128)(2,1)} %copy-done.7, ...), custom_call_target="tpu_custom_call" | custom-call | tf_op jit(solution)/shard_map/attend/pallas_call | solution.py:289
  132.1 4.9 %slice.216 = bf16[32,96,768]{2,1,0:T(8,128)(2,1)S(1)} slice(bf16[32,216,768]{2,1,0:T(8,128)(2,1)} %all-gather.2.cloned.1.call-done), slice={[0:32], [120:216], [0:768]} | slice | bytes 9437184 | tf_op jit(solution)/shard_map/slice | solution.py:400
  137.1 7.1 %fusion.89 = (bf16[3072]{0:T(1024)(128)(2,1)}, bf16[512,3072]{1,0:T(8,128)(2,1)S(1)}) fusion(f32[512,3072]{1,0:T(8,128)S(1)} %fusion.46, f32[3072]{0:T(1024)S(1)} %copy-done.40, bf16[512,768]{1,0:T(8,128)(2,1)S(1)} %copy-done.27, bf16[3072,768]{1,0:T(8,128)(2,1)S(1)} %bitcast.257), kind=kOutput, calls=%fused_computation.237 | convolution fusion | flops 2450519040 | bytes 14960640 | tf_op jit(solution)/shard_map/dot_general | solution.py:47
  157.9 5.2 %add_add_fusion = f32[512,768]{1,0:T(8,128)} fusion(f32[512,768]{1,0:T(8,128)S(1)} %get-tuple-element.188, bf16[3072,768]{1,0:T(8,128)(2,1)S(1)} %bitcast.258, f32[768]{0:T(1024)S(1)} %get-tuple-element.115, f32[512,3072]{1,0:T(8,128)S(1)} %fusion.46, f32[3072]{0:T(1024)S(1)} %copy-done.40), kind=kOutput, calls=%fused_computation.71 | convolution fusion | flops 2432434176 | bytes 14171136 | tf_op jit(solution)/shard_map/dot_general | solution.py:444
  165.4 6.0 %far_back.2 = (f32[1,256,768]{2,1,0:T(8,128)}, bf16[1,2,256,768]{3,2,1,0:T(8,128)(2,1)}) custom-call(s32[1]{0:T(128)} %bitcast.limit, bf16[2,256,768]{2,1,0:T(8,128)(2,1)} %bitcast.244, bf16[1,256,1536]{2,1,0:T(8,128)(2,1)} %copy-done.8, bf16[1,256,1536]{2,1,0:T(8,128)(2,1)} %copy-done.8, bf16[2,256,768]{2,1,0:T(8,128)(2,1)} %bitcast.251, ...), custom_call_target="tpu_custom_call" | custom-call | tf_op jit(solution)/shard_map/far_back/pallas_call | solution.py:314
  171.4 6.4 %own_back.2 = (bf16[1,256,768]{2,1,0:T(8,128)(2,1)}, f32[1,1,768]{2,1,0:T(1,128)}, f32[1,2,256,768]{3,2,1,0:T(8,128)}) custom-call(bf16[2,256,768]{2,1,0:T(8,128)(2,1)} %bitcast.245, bf16[2,256,1536]{2,1,0:T(8,128)(2,1)} %bitcast.239, bf16[2,256,1536]{2,1,0:T(8,128)(2,1)} %bitcast.240, bf16[2,256,768]{2,1,0:T(8,128)(2,1)} %bitcast.252, ...), custom_call_target="tpu_custom_call" | custom-call | tf_op jit(solution)/shard_map/own_back/pallas_call | solution.py:340
  179.6 6.2 %far_back.3 = (f32[1,256,768]{2,1,0:T(8,128)}, bf16[1,2,256,768]{3,2,1,0:T(8,128)(2,1)}) custom-call(s32[1]{0:T(128)} %bitcast.limit, bf16[2,256,768]{2,1,0:T(8,128)(2,1)} %bitcast.246, bf16[1,256,1536]{2,1,0:T(8,128)(2,1)} %copy-done.7, bf16[1,256,1536]{2,1,0:T(8,128)(2,1)} %copy-done.7, bf16[2,256,768]{2,1,0:T(8,128)(2,1)} %bitcast.253, ...), custom_call_target="tpu_custom_call" | custom-call | tf_op jit(solution)/shard_map/far_back/pallas_call | solution.py:314
  185.8 6.3 %own_back.3 = (bf16[2,256,768]{2,1,0:T(8,128)(2,1)}, f32[1,2,256,768]{3,2,1,0:T(8,128)}, f32[1,1,768]{2,1,0:T(1,128)}) fusion(bf16[2,256,768]{2,1,0:T(8,128)(2,1)} %constant_dynamic-update-slice_fusion.3, bf16[2,256,768]{2,1,0:T(8,128)(2,1)S(1)} %bitcast.247, bf16[2,256,1536]{2,1,0:T(8,128)(2,1)S(1)} %bitcast.241, bf16[2,256,768]{2,1,0:T(8,128)(2,1)} %bitcast.254, ...), kind=kCustom, calls=%fused_computation.203 | custom fusion | bytes 6306816 | tf_op jit(solution)/shard_map/own_back/pallas_call | solution.py:340
  198.6 8.7 %convolution_convert_fusion = bf16[3072,768]{1,0:T(8,128)(2,1)} fusion(bf16[512,768]{1,0:T(8,128)(2,1)S(1)} %copy-done.28, f32[512,3072]{1,0:T(8,128)} %copy-done.55, f32[3072]{0:T(1024)S(1)} %copy-done.41), kind=kOutput, calls=%fused_computation.9 | convolution fusion | flops 2434007040 | bytes 11808768 | tf_op jit(solution)/shard_map/dot_general | solution.py:41
  217.4 9.0 %collective-permute-done.14 = bf16[4,2,24,3072]{3,2,1,0:T(8,128)(2,1)} collective-permute-done((bf16[4,2,24,3072]{3,2,1,0:T(8,128)(2,1)}, bf16[4,2,24,3072]{3,2,1,0:T(8,128)(2,1)}, u32[]{:S(2)}, u32[]{:S(2)}) %collective-permute-start.14) | collective-permute-done | bytes 1179680 | tf_op jit(solution)/shard_map/ppermute | solution.py:70
  229.2 4.4 %collective-permute-done.12 = bf16[1,2,256,768]{3,2,1,0:T(8,128)(2,1)} collective-permute-done((bf16[1,2,256,768]{3,2,1,0:T(8,128)(2,1)}, bf16[1,2,256,768]{3,2,1,0:T(8,128)(2,1)}, u32[]{:S(2)}, u32[]{:S(2)}) %collective-permute-start.12) | collective-permute-done | bytes 786464 | tf_op jit(solution)/shard_map/ppermute | solution.py:469
  233.6 15.5 %collective-permute-done.13 = bf16[1,2,256,768]{3,2,1,0:T(8,128)(2,1)} collective-permute-done((bf16[1,2,256,768]{3,2,1,0:T(8,128)(2,1)}, bf16[1,2,256,768]{3,2,1,0:T(8,128)(2,1)}, u32[]{:S(2)}, u32[]{:S(2)}) %collective-permute-start.13) | collective-permute-done | bytes 786464 | tf_op jit(solution)/shard_map/ppermute | solution.py:469
  275.8 9.8 %collective-permute-done.29 = bf16[2,24,3072]{2,1,0:T(8,128)(2,1)S(1)} collective-permute-done((bf16[2,24,3072]{2,1,0:T(8,128)(2,1)S(1)}, bf16[2,24,3072]{2,1,0:T(8,128)(2,1)S(1)}, u32[]{:S(2)}, u32[]{:S(2)}) %collective-permute-start.29) | collective-permute-done | bytes 294944 | tf_op jit(solution)/shard_map/ppermute | solution.py:70
  288.6 19.8 %collective-permute-done.30 = bf16[2,24,3072]{2,1,0:T(8,128)(2,1)S(1)} collective-permute-done((bf16[2,24,3072]{2,1,0:T(8,128)(2,1)S(1)}, bf16[2,24,3072]{2,1,0:T(8,128)(2,1)S(1)}, u32[]{:S(2)}, u32[]{:S(2)}) %collective-permute-start.30) | collective-permute-done | bytes 294944 | tf_op jit(solution)/shard_map/ppermute | solution.py:70
  311.1 5.5 %collective-permute-done.32 = bf16[24,3072]{1,0:T(8,128)(2,1)S(1)} collective-permute-done((bf16[24,3072]{1,0:T(8,128)(2,1)S(1)}, bf16[24,3072]{1,0:T(8,128)(2,1)S(1)}, u32[]{:S(2)}, u32[]{:S(2)}) %collective-permute-start.32) | collective-permute-done | bytes 147488 | tf_op jit(solution)/shard_map/ppermute | solution.py:70
  317.3 4.5 %collective-permute-done.25 = bf16[4,24,1536]{2,1,0:T(8,128)(2,1)S(1)} collective-permute-done((bf16[4,24,1536]{2,1,0:T(8,128)(2,1)S(1)}, bf16[4,24,1536]{2,1,0:T(8,128)(2,1)S(1)}, u32[]{:S(2)}, u32[]{:S(2)}) %collective-permute-start.25) | collective-permute-done | bytes 294944 | tf_op jit(solution)/shard_map/ppermute | solution.py:70
  335.0 6.1 %collective-permute-done.19 = bf16[4,2,24,896]{3,2,1,0:T(8,128)(2,1)S(1)} collective-permute-done((bf16[4,2,24,896]{3,2,1,0:T(8,128)(2,1)S(1)}, bf16[4,2,24,896]{3,2,1,0:T(8,128)(2,1)S(1)}, u32[]{:S(2)}, u32[]{:S(2)}) %collective-permute-start.19) | collective-permute-done | bytes 344096 | tf_op jit(solution)/shard_map/ppermute | solution.py:70
  (312 shorter events, 169.0 us)
Async XLA Ops:
  7.2 117.8 %all-gather.2.cloned.1.call-start = ((), (), s32[]{:S(2)}) async-start(), calls=%async_computation.1 | async-start | bytes 11280384 | tf_op jit(solution)/shard_map/all_gather | solution.py:384
  12.0 10.8 %collective-permute-start.10 = (bf16[216,768]{1,0:T(8,128)(2,1)S(1)}, bf16[216,768]{1,0:T(8,128)(2,1)S(1)}, u32[]{:S(2)}, u32[]{:S(2)}) collective-permute-start(bf16[216,768]{1,0:T(8,128)(2,1)S(1)} %constant_dynamic-update-slice_fusion), channel_id=1, source_target_pairs={{0,1},{1,0},{2,3},{3,2},{4,5},{5,4},{6,7},{7,6},{8,9},{9,8},{10,11... | collective-permute-start | bytes 995336 | tf_op jit(solution)/shard_map/ppermute | solution.py:70
  23.8 333.4 %reduce-scatter.2.cloned.1.call-start = ((), (), s32[]{:S(2)}) async-start(), calls=%async_computation.2 | async-start | bytes 4866048 | tf_op jit(solution)/shard_map/reduce_scatter | solution.py:161
  24.3 8.0 %collective-permute-start.2 = (bf16[24,2432]{1,0:T(8,128)(2,1)S(1)}, bf16[24,2432]{1,0:T(8,128)(2,1)S(1)}, u32[]{:S(2)}, u32[]{:S(2)}) collective-permute-start(bf16[24,2432]{1,0:T(8,128)(2,1)S(1)} %pad_maximum_fusion.17), channel_id=1, source_target_pairs={{0,8},{1,9},{2,10},{3,11},{4,12},{5,13},{6,14},{7,15},{8,16},{9,17... | collective-permute-start | bytes 350216 | tf_op jit(solution)/shard_map/ppermute | solution.py:70
  26.2 9.5 %collective-permute-start.1 = (bf16[24,2432]{1,0:T(8,128)(2,1)S(1)}, bf16[24,2432]{1,0:T(8,128)(2,1)S(1)}, u32[]{:S(2)}, u32[]{:S(2)}) collective-permute-start(bf16[24,2432]{1,0:T(8,128)(2,1)S(1)} %pad_maximum_fusion.17), channel_id=1, source_target_pairs={{0,16},{1,17},{2,18},{3,19},{4,20},{5,21},{6,22},{7,23},{8,24},{9,... | collective-permute-start | bytes 350216 | tf_op jit(solution)/shard_map/ppermute | solution.py:70
  36.2 12.0 %collective-permute-start.3 = (bf16[4,24,1152]{2,1,0:T(8,128)(2,1)S(1)}, bf16[4,24,1152]{2,1,0:T(8,128)(2,1)S(1)}, u32[]{:S(2)}, u32[]{:S(2)}) collective-permute-start(bf16[4,24,1152]{2,1,0:T(8,128)(2,1)S(1)} %pad_maximum_fusion.15), channel_id=1, source_target_pairs={{0,4},{1,5},{2,6},{3,7},{4,0},{5,1},{6,2},{7,3},{8,12},{9,13},{10,... | collective-permute-start | bytes 663560 | tf_op jit(solution)/shard_map/ppermute | solution.py:70
  37.8 12.1 %collective-permute-start.5 = (bf16[4,24,1280]{2,1,0:T(8,128)(2,1)S(1)}, bf16[4,24,1280]{2,1,0:T(8,128)(2,1)S(1)}, u32[]{:S(2)}, u32[]{:S(2)}) collective-permute-start(bf16[4,24,1280]{2,1,0:T(8,128)(2,1)S(1)} %pad_maximum_fusion.12), channel_id=1, source_target_pairs={{0,1},{1,0},{2,3},{3,2},{4,5},{5,4},{6,7},{7,6},{8,9},{9,8},{10,11... | collective-permute-start | bytes 737288 | tf_op jit(solution)/shard_map/ppermute | solution.py:70
  48.3 11.7 %collective-permute-start.4 = (bf16[4,2,24,1152]{3,2,0,1:T(8,128)(2,1)S(1)}, bf16[4,2,24,1152]{3,2,0,1:T(8,128)(2,1)S(1)}, u32[]{:S(2)}, u32[]{:S(2)}) collective-permute-start(bf16[4,2,24,1152]{3,2,0,1:T(8,128)(2,1)S(1)} %pad_maximum_fusion.11), channel_id=1, source_target_pairs={{0,1},{1,0},{2,3},{3,2},{4,5},{5,4},{6,7},{7,6},{8,9},{9,8},{10,11... | collective-permute-start | bytes 1327112 | tf_op jit(solution)/shard_map/ppermute | solution.py:70
  50.0 12.6 %collective-permute-start.6 = (bf16[4,2,24,1280]{3,2,1,0:T(8,128)(2,1)S(1)}, bf16[4,2,24,1280]{3,2,1,0:T(8,128)(2,1)S(1)}, u32[]{:S(2)}, u32[]{:S(2)}) collective-permute-start(bf16[4,2,24,1280]{3,2,1,0:T(8,128)(2,1)S(1)} %pad_maximum_fusion.10), channel_id=1, source_target_pairs={{0,4},{1,5},{2,6},{3,7},{4,0},{5,1},{6,2},{7,3},{8,12},{9,13},{10,... | collective-permute-start | bytes 1474568 | tf_op jit(solution)/shard_map/ppermute | solution.py:70
  79.5 21.0 %collective-permute-start.8 = (bf16[1,256,1536]{2,1,0:T(8,128)(2,1)}, bf16[1,256,1536]{2,1,0:T(8,128)(2,1)S(1)}, u32[]{:S(2)}, u32[]{:S(2)}) collective-permute-start(bf16[1,256,1536]{2,1,0:T(8,128)(2,1)} %maximum_bitcast_fusion), channel_id=1, source_target_pairs={{0,1},{2,3},{4,5},{6,7},{8,9},{10,11},{12,13},{14,15},{16,17},{18,... | collective-permute-start | bytes 2359304 | tf_op jit(solution)/shard_map/ppermute | solution.py:421
  83.3 33.2 %collective-permute-start.9 = (bf16[1,256,1536]{2,1,0:T(8,128)(2,1)}, bf16[1,256,1536]{2,1,0:T(8,128)(2,1)S(1)}, u32[]{:S(2)}, u32[]{:S(2)}) collective-permute-start(bf16[1,256,1536]{2,1,0:T(8,128)(2,1)} %maximum_bitcast_fusion.1), channel_id=1, source_target_pairs={{0,1},{2,3},{4,5},{6,7},{8,9},{10,11},{12,13},{14,15},{16,17},{18,... | collective-permute-start | bytes 2359304 | tf_op jit(solution)/shard_map/ppermute | solution.py:421
  152.0 11.1 %collective-permute-start.11 = (bf16[4,2,2,24,3072]{4,3,2,0,1:T(8,128)(2,1)S(1)}, bf16[4,2,2,24,3072]{4,3,2,0,1:T(8,128)(2,1)S(1)}, u32[]{:S(2)}, u32[]{:S(2)}) collective-permute-start(bf16[4,2,2,24,3072]{4,3,2,0,1:T(8,128)(2,1)S(1)} %bitcast.263), channel_id=1, source_target_pairs={{0,2},{1,3},{2,0},{3,1},{4,6},{5,7},{6,4},{7,5},{8,10},{9,11},{10,... | collective-permute-start | bytes 7077896 | tf_op jit(solution)/shard_map/ppermute | solution.py:70
  196.6 17.9 %collective-permute-start.15 = (bf16[4,2,2,24,1536]{4,3,2,1,0:T(8,128)(2,1)}, bf16[4,2,2,24,1536]{4,3,2,1,0:T(8,128)(2,1)}, u32[]{:S(2)}, u32[]{:S(2)}) collective-permute-start(bf16[4,2,2,24,1536]{4,3,2,1,0:T(8,128)(2,1)} %pad_maximum_fusion.4), channel_id=1, source_target_pairs={{0,2},{1,3},{2,0},{3,1},{4,6},{5,7},{6,4},{7,5},{8,10},{9,11},{10,... | collective-permute-start | bytes 3538952 | tf_op jit(solution)/shard_map/ppermute | solution.py:70
  198.4 28.0 %collective-permute-start.14 = (bf16[4,2,24,3072]{3,2,1,0:T(8,128)(2,1)}, bf16[4,2,24,3072]{3,2,1,0:T(8,128)(2,1)}, u32[]{:S(2)}, u32[]{:S(2)}) collective-permute-start(bf16[4,2,24,3072]{3,2,1,0:T(8,128)(2,1)} %dynamic-slice_bitcast_fusion.2), channel_id=1, source_target_pairs={{0,4},{1,5},{2,6},{3,7},{4,0},{5,1},{6,2},{7,3},{8,12},{9,13},{10,... | collective-permute-start | bytes 3538952 | tf_op jit(solution)/shard_map/ppermute | solution.py:70
  211.0 22.6 %collective-permute-start.12 = (bf16[1,2,256,768]{3,2,1,0:T(8,128)(2,1)}, bf16[1,2,256,768]{3,2,1,0:T(8,128)(2,1)}, u32[]{:S(2)}, u32[]{:S(2)}) collective-permute-start(bf16[1,2,256,768]{3,2,1,0:T(8,128)(2,1)} %get-tuple-element.47), channel_id=1, source_target_pairs={{1,0},{3,2},{5,4},{7,6},{9,8},{11,10},{13,12},{15,14},{17,16},{19,... | collective-permute-start | bytes 2359304 | tf_op jit(solution)/shard_map/ppermute | solution.py:469
  212.3 36.8 %collective-permute-start.13 = (bf16[1,2,256,768]{3,2,1,0:T(8,128)(2,1)}, bf16[1,2,256,768]{3,2,1,0:T(8,128)(2,1)}, u32[]{:S(2)}, u32[]{:S(2)}) collective-permute-start(bf16[1,2,256,768]{3,2,1,0:T(8,128)(2,1)} %get-tuple-element.49), channel_id=1, source_target_pairs={{1,0},{3,2},{5,4},{7,6},{9,8},{11,10},{13,12},{15,14},{17,16},{19,... | collective-permute-start | bytes 2359304 | tf_op jit(solution)/shard_map/ppermute | solution.py:469
  266.7 42.7 %collective-permute-start.24 = (bf16[4,2,24,1536]{3,2,1,0:T(8,128)(2,1)S(1)}, bf16[4,2,24,1536]{3,2,1,0:T(8,128)(2,1)S(1)}, u32[]{:S(2)}, u32[]{:S(2)}) collective-permute-start(bf16[4,2,24,1536]{3,2,1,0:T(8,128)(2,1)S(1)} %dynamic-slice_bitcast_fusion.3), channel_id=1, source_target_pairs={{0,4},{1,5},{2,6},{3,7},{4,0},{5,1},{6,2},{7,3},{8,12},{9,13},{10,... | collective-permute-start | bytes 1769480 | tf_op jit(solution)/shard_map/ppermute | solution.py:70
  268.6 17.0 %collective-permute-start.29 = (bf16[2,24,3072]{2,1,0:T(8,128)(2,1)S(1)}, bf16[2,24,3072]{2,1,0:T(8,128)(2,1)S(1)}, u32[]{:S(2)}, u32[]{:S(2)}) collective-permute-start(bf16[2,24,3072]{2,1,0:T(8,128)(2,1)S(1)} %get-tuple-element.144), channel_id=1, source_target_pairs={{0,8},{1,9},{2,10},{3,11},{4,12},{5,13},{6,14},{7,15},{8,16},{9,17... | collective-permute-start | bytes 884744 | tf_op jit(solution)/shard_map/ppermute | solution.py:70
  269.9 18.8 %collective-permute-start.31 = (bf16[2,24,3072]{2,1,0:T(8,128)(2,1)S(1)}, bf16[2,24,3072]{2,1,0:T(8,128)(2,1)S(1)}, u32[]{:S(2)}, u32[]{:S(2)}) collective-permute-start(bf16[2,24,3072]{2,1,0:T(8,128)(2,1)S(1)} %get-tuple-element.145), channel_id=1, source_target_pairs={{0,24},{1,25},{2,26},{3,27},{4,28},{5,29},{6,30},{7,31},{8,0},{9,1... | collective-permute-start | bytes 884744 | tf_op jit(solution)/shard_map/ppermute | solution.py:70
  272.5 36.0 %collective-permute-start.30 = (bf16[2,24,3072]{2,1,0:T(8,128)(2,1)S(1)}, bf16[2,24,3072]{2,1,0:T(8,128)(2,1)S(1)}, u32[]{:S(2)}, u32[]{:S(2)}) collective-permute-start(bf16[2,24,3072]{2,1,0:T(8,128)(2,1)S(1)} %get-tuple-element.146), channel_id=1, source_target_pairs={{0,16},{1,17},{2,18},{3,19},{4,20},{5,21},{6,22},{7,23},{8,24},{9,... | collective-permute-start | bytes 884744 | tf_op jit(solution)/shard_map/ppermute | solution.py:70
  272.9 52.9 %collective-permute-start.16 = (bf16[4,2,2,24,1664]{4,3,2,1,0:T(8,128)(2,1)S(1)}, bf16[4,2,2,24,1664]{4,3,2,1,0:T(8,128)(2,1)S(1)}, u32[]{:S(2)}, u32[]{:S(2)}) collective-permute-start(bf16[4,2,2,24,1664]{4,3,2,1,0:T(8,128)(2,1)S(1)} %pad_maximum_fusion.3), channel_id=1, source_target_pairs={{0,2},{1,3},{2,0},{3,1},{4,6},{5,7},{6,4},{7,5},{8,10},{9,11},{10,... | collective-permute-start | bytes 3833864 | tf_op jit(solution)/shard_map/ppermute | solution.py:70
  309.6 12.2 %collective-permute-start.25 = (bf16[4,24,1536]{2,1,0:T(8,128)(2,1)S(1)}, bf16[4,24,1536]{2,1,0:T(8,128)(2,1)S(1)}, u32[]{:S(2)}, u32[]{:S(2)}) collective-permute-start(bf16[4,24,1536]{2,1,0:T(8,128)(2,1)S(1)} %dynamic-slice_bitcast_fusion.12), channel_id=1, source_target_pairs={{0,1},{1,0},{2,3},{3,2},{4,5},{5,4},{6,7},{7,6},{8,9},{9,8},{10,11... | collective-permute-start | bytes 884744 | tf_op jit(solution)/shard_map/ppermute | solution.py:70
  331.2 9.9 %collective-permute-start.19 = (bf16[4,2,24,896]{3,2,1,0:T(8,128)(2,1)S(1)}, bf16[4,2,24,896]{3,2,1,0:T(8,128)(2,1)S(1)}, u32[]{:S(2)}, u32[]{:S(2)}) collective-permute-start(bf16[4,2,24,896]{3,2,1,0:T(8,128)(2,1)S(1)} %dynamic-slice_bitcast_fusion.8), channel_id=1, source_target_pairs={{0,4},{1,5},{2,6},{3,7},{4,0},{5,1},{6,2},{7,3},{8,12},{9,13},{10,... | collective-permute-start | bytes 1032200 | tf_op jit(solution)/shard_map/ppermute | solution.py:70
  333.9 8.7 %collective-permute-start.18 = (bf16[4,24,768]{2,1,0:T(8,128)(2,1)S(1)}, bf16[4,24,768]{2,1,0:T(8,128)(2,1)S(1)}, u32[]{:S(2)}, u32[]{:S(2)}) collective-permute-start(bf16[4,24,768]{2,1,0:T(8,128)(2,1)S(1)} %dynamic-slice_bitcast_fusion.16), channel_id=1, source_target_pairs={{0,4},{1,5},{2,6},{3,7},{4,0},{5,1},{6,2},{7,3},{8,12},{9,13},{10,... | collective-permute-start | bytes 442376 | tf_op jit(solution)/shard_map/ppermute | solution.py:70
  (67 other events, 463.4 us)
Sparse Core Ops, SparseCore 0:
  24.0 90.5 all-gather.1
  207.5 118.0 reduce-scatter.1
